TPU v7x, 256 devices: a whole 4x4x8 slice. The times are simulated.
256 devices in a mesh: dp: 4 (over x), space: 16 (over z_lo, y), tm: 4 (over z_hi, core).
Axes of the slice: x: 4, y: 4, z: 8 (z_hi: 2, z_lo: 4; z = z_hi * 4 + z_lo), core: 2. Of those that a mesh axis runs over, the one named last changes fastest.
Arguments:
- inputs: bfloat16 [4, 32, 64, 4096], P('dp', 'tm', None, 'space'), may hold values from -6 to 6
- grad_out: bfloat16 [4, 32, 64, 4096], P('dp', 'tm', None, 'space'), may hold values from -6 to 6
- conv_w: bfloat16 [2, 128, 64], replicated, may hold values from -0.5 to 0.5
- conv_b: float32 [128], replicated, may hold values from -3 to 3
- mix_w: bfloat16 [3, 64, 64], replicated, may hold values from -0.4375 to 0.4375
- mix_b: float32 [64], replicated, may hold values from -3 to 3
- adj_tiles: bfloat16 [32, 8, 128, 128], P('space'), may hold values from -0.1875 to 0.1875
- tile_cols: int32 [32, 8], P('space'), may hold values from 0 to 9, as said below
- send_rows: int32 [16, 16, 64], P('space'), may hold values from 0 to 255
- counts: int32 [16, 16], P('space'), may hold values from 0 to 64, as said below
Outputs:
- outputs: bfloat16 [4, 32, 64, 4096], P('dp', 'tm', None, 'space')
- grad_inputs: bfloat16 [4, 32, 64, 4096], P('dp', 'tm', None, 'space')
- grad_conv_w: float32 [2, 128, 64], replicated
- grad_conv_b: float32 [128], replicated
- grad_mix_w: float32 [3, 64, 64], replicated
- grad_mix_b: float32 [64], replicated
Inputs may be any that keep to these rules, and one draw needn't show every extreme that they name: counts[s, s] = 0; counts[0, 1] = 64. `tile_cols`: column blocks below 2 are the part's own sensor blocks, 2 + i the i-th block of 128 received slots in order of source part and slot; in each row block the first 4 ids are below 2, the others are not.
All inputs are finite; a program needn't handle non-finite values.
Results may differ from a plain program's by a relative error of at most 0.0058.
Values may be sent and summed in bfloat16 or wider, within the bound.
A program may use at most 64 MiB of HBM per device.

v0:
```python
import math

import jax
import jax.numpy as jnp
from jax import lax
from jax.sharding import PartitionSpec as P

DILATION_SIZE = 2


def from_behind(value, axis, steps):
    count = lax.axis_size(axis)
    leading, last = (max(0, -steps), min(count, count - steps))
    return lax.ppermute(value, axis, [(source, source + steps) for source in range(leading, last)])


def slot_mask(counts, slot_count, dtype):
    slots = lax.broadcasted_iota(jnp.int32, (counts.shape[1], slot_count), 1)
    return (slots < counts[0][:, None]).astype(dtype)


def pack_rows(field, send_rows, live_slots):
    picked = field[:, :, send_rows[0]] * live_slots
    return picked.reshape(field.shape[0], field.shape[1], -1)


def tile_product(extended, adj_tiles, tile_cols):
    timestep_count, chan_count = (extended.shape[0], extended.shape[1])
    blocks = extended.reshape(timestep_count, chan_count, -1, adj_tiles.shape[2])
    picked = blocks[:, :, tile_cols]
    return jnp.einsum("tcrkj,rkij->tcri", picked, adj_tiles, preferred_element_type=jnp.float32)


def forward_start(field, send_rows, live_slots):
    packed = pack_rows(field, send_rows, live_slots)
    own_part = None
    return (packed, own_part)


def forward_finish(field, received, adj_tiles, tile_cols):
    total = tile_product(jnp.concatenate([field, received], 2), adj_tiles, tile_cols)
    return total.reshape(field.shape).astype(jnp.bfloat16)


def back_start(grad, adj_tiles, tile_cols, send_rows):
    timestep_count, chan_count, sensor_count = grad.shape
    tile_size = adj_tiles.shape[2]
    row_blocks = sensor_count // tile_size
    half_slots = tile_cols.shape[1] // 2
    halo_blocks = send_rows.shape[1] * send_rows.shape[2] // tile_size
    blocks = grad.reshape(timestep_count, chan_count, row_blocks, tile_size)
    remote_terms = jnp.einsum(
        "tcri,rkij->tcrkj", blocks, adj_tiles[:, half_slots:], preferred_element_type=jnp.float32
    )
    remote_sums = jnp.zeros((timestep_count, chan_count, halo_blocks, tile_size), jnp.float32)
    remote_sums = remote_sums.at[:, :, tile_cols[:, half_slots:] - row_blocks].add(remote_terms)
    return remote_sums.reshape(timestep_count, chan_count, -1).astype(jnp.bfloat16)


def back_finish(grad, returned, adj_tiles, tile_cols, send_rows, live_slots):
    timestep_count, chan_count, sensor_count = grad.shape
    tile_size = adj_tiles.shape[2]
    row_blocks = sensor_count // tile_size
    half_slots = tile_cols.shape[1] // 2
    blocks = grad.reshape(timestep_count, chan_count, row_blocks, tile_size)
    own_terms = jnp.einsum(
        "tcri,rkij->tcrkj", blocks, adj_tiles[:, :half_slots], preferred_element_type=jnp.float32
    )
    total = jnp.zeros((timestep_count, chan_count, row_blocks, tile_size), jnp.float32)
    total = total.at[:, :, tile_cols[:, :half_slots]].add(own_terms).reshape(grad.shape)
    returned = returned.reshape(
        timestep_count, chan_count, send_rows.shape[1], send_rows.shape[2]
    ).astype(jnp.float32)
    return total.at[:, :, send_rows[0]].add(returned * live_slots.astype(jnp.float32))


def mixing_grads(sample_grad, fields):
    grad_mix_w = jnp.stack(
        [
            jnp.einsum("ton,tcn->oc", sample_grad, item, preferred_element_type=jnp.float32)
            for item in fields
        ]
    )
    grad_mix_b = jnp.sum(sample_grad.astype(jnp.float32), axis=(0, 2))
    return (grad_mix_w, grad_mix_b)


def body(inputs, grad_out, conv_w, conv_b, mix_w, mix_b, adj_tiles, tile_cols, send_rows, counts):
    sample_input = inputs[0]
    sample_grad = grad_out[0]
    timestep_count, chan_count, sensor_count = sample_input.shape
    live_slots = slot_mask(counts, send_rows.shape[2], jnp.bfloat16)
    prior_border_slice = from_behind(sample_input[timestep_count - DILATION_SIZE :], "tm", 1)
    preceding_window = jnp.concatenate(
        [prior_border_slice, sample_input[: timestep_count - DILATION_SIZE]], 0
    )
    preact = jnp.einsum("oc,tcn->ton", conv_w[1], sample_input, preferred_element_type=jnp.float32)
    preact = preact + jnp.einsum(
        "oc,tcn->ton", conv_w[0], preceding_window, preferred_element_type=jnp.float32
    )
    preact = preact + conv_b[None, :, None]
    filtered = jnp.tanh(preact[:, :chan_count])
    gating = jax.nn.sigmoid(preact[:, chan_count:])
    hidden = (filtered * gating).astype(jnp.bfloat16)
    grad_float = sample_grad.astype(jnp.float32)
    packed_one, early_one = forward_start(hidden, send_rows, live_slots)
    received_one = lax.all_to_all(packed_one, "space", split_axis=2, concat_axis=2, tiled=True)
    hop_one = forward_finish(hidden, received_one, adj_tiles, tile_cols)
    packed_two, early_two = forward_start(hop_one, send_rows, live_slots)
    received_two = lax.all_to_all(packed_two, "space", split_axis=2, concat_axis=2, tiled=True)
    hop_two = forward_finish(hop_one, received_two, adj_tiles, tile_cols)
    fields = (hidden, hop_one, hop_two)
    grad_mix_w, grad_mix_b = mixing_grads(sample_grad, fields)
    back_two = jnp.einsum(
        "oc,ton->tcn", mix_w[2], sample_grad, preferred_element_type=jnp.float32
    ).astype(jnp.bfloat16)
    returned_two = lax.all_to_all(
        back_start(back_two, adj_tiles, tile_cols, send_rows),
        "space",
        split_axis=2,
        concat_axis=2,
        tiled=True,
    )
    back_one = jnp.einsum("oc,ton->tcn", mix_w[1], sample_grad, preferred_element_type=jnp.float32)
    back_one = (
        back_one + back_finish(back_two, returned_two, adj_tiles, tile_cols, send_rows, live_slots)
    ).astype(jnp.bfloat16)
    returned_one = lax.all_to_all(
        back_start(back_one, adj_tiles, tile_cols, send_rows),
        "space",
        split_axis=2,
        concat_axis=2,
        tiled=True,
    )
    back_hidden = jnp.einsum(
        "oc,ton->tcn", mix_w[0], sample_grad, preferred_element_type=jnp.float32
    )
    back_hidden = back_hidden + back_finish(
        back_one, returned_one, adj_tiles, tile_cols, send_rows, live_slots
    )
    mixed = sample_input.astype(jnp.float32) + mix_b[None, :, None]
    for index in range(3):
        mixed = mixed + jnp.einsum(
            "oc,tcn->ton", mix_w[index], fields[index], preferred_element_type=jnp.float32
        )
    outputs = mixed.astype(jnp.bfloat16)[None]
    grad_filter = back_hidden * (1.0 - filtered * filtered) * gating
    grad_gate = back_hidden * filtered * gating * (1.0 - gating)
    backward_preactivation = jnp.concatenate([grad_filter, grad_gate], 1).astype(jnp.bfloat16)
    next_border_slice = from_behind(backward_preactivation[:DILATION_SIZE], "tm", -1)
    following_window = jnp.concatenate(
        [backward_preactivation[DILATION_SIZE:], next_border_slice], 0
    )
    grad_inputs = grad_float + jnp.einsum(
        "oc,ton->tcn", conv_w[1], backward_preactivation, preferred_element_type=jnp.float32
    )
    grad_inputs = grad_inputs + jnp.einsum(
        "oc,ton->tcn", conv_w[0], following_window, preferred_element_type=jnp.float32
    )
    grad_inputs = grad_inputs.astype(jnp.bfloat16)[None]
    grad_conv_w = jnp.stack(
        [
            jnp.einsum(
                "ton,tcn->oc",
                backward_preactivation,
                preceding_window,
                preferred_element_type=jnp.float32,
            ),
            jnp.einsum(
                "ton,tcn->oc",
                backward_preactivation,
                sample_input,
                preferred_element_type=jnp.float32,
            ),
        ]
    )
    grad_conv_b = jnp.sum(backward_preactivation.astype(jnp.float32), axis=(0, 2))
    grad_conv_w, grad_conv_b, grad_mix_w, grad_mix_b = lax.psum(
        (grad_conv_w, grad_conv_b, grad_mix_w, grad_mix_b), ("dp", "space", "tm")
    )
    cell_count = (
        inputs.shape[0]
        * timestep_count
        * sensor_count
        * lax.axis_size("dp")
        * lax.axis_size("space")
        * lax.axis_size("tm")
    )
    scale = 1.0 / math.sqrt(cell_count)
    return (
        outputs,
        grad_inputs,
        grad_conv_w * scale,
        grad_conv_b * scale,
        grad_mix_w * scale,
        grad_mix_b * scale,
    )


def solution(mesh):
    in_specs = (
        P("dp", "tm", None, "space"),
        P("dp", "tm", None, "space"),
        P(),
        P(),
        P(),
        P(),
        P("space", None, None, None),
        P("space", None),
        P("space", None, None),
        P("space", None),
    )
    out_specs = (P("dp", "tm", None, "space"), P("dp", "tm", None, "space"), P(), P(), P(), P())
    return jax.shard_map(body, mesh=mesh, in_specs=in_specs, out_specs=out_specs, check_vma=False)
```

profile of v0, /device:TPU:1, one launch (start us, length us, event | category | flops | bytes accessed | tf_op | source)
XLA Modules:
  0.0 680.7 jit_solution(10881315894750508709)
XLA Ops:
  12.5 3.5 scatter_fusion.1
  19.6 9.2 %all-to-all-start.2 = ((bf16[16,2,16384]{2,1,0:T(2,128)(2,1)}), bf16[16,2,16384]{2,1,0:T(2,128)(2,1)}, u32[]{:S(2)}, u32[]{:S(2)}) async-start(bf16[16,2,16384]{2,1,0:T(2,128)(2,1)} %reshape.258), calls=%async_computation.2 | async-start | bytes 2097152 | tf_op jit(solution)/shard_map/all_to_all | solution.py:117
  32.5 18.7 %all-to-all-done.2 = bf16[16,2,16384]{2,1,0:T(2,128)(2,1)} async-done(((bf16[16,2,16384]{2,1,0:T(2,128)(2,1)}), bf16[16,2,16384]{2,1,0:T(2,128)(2,1)}, u32[]{:S(2)}, u32[]{:S(2)}) %all-to-all-start.2) | async-done | bytes 1048608 | tf_op jit(solution)/shard_map/all_to_all | solution.py:117
  51.2 3.8 reshape.259
  55.0 3.1 convert_multiply_fusion.1
  58.1 71.3 %scatter_fusion.2 = f32[8,64,256]{1,0,2:T(8,128)S(1)} fusion(f32[8,64,256]{1,0,2:T(8,128)S(1)} %copy.84, s32[1024]{0:T(1024)S(1)} %reshape.131, f32[1024,8,64]{2,1,0:T(8,128)} %bitcast.273), kind=kCustom, calls=%fused_computation.6 | custom fusion | flops 524288 | bytes 6295552 | tf_op jit(solution)/shard_map/scatter-add | solution.py:74
  132.5 3.5 scatter_fusion.4
  141.6 7.7 %all-to-all-start.3 = ((bf16[16,2,16384]{2,1,0:T(2,128)(2,1)}), bf16[16,2,16384]{2,1,0:T(2,128)(2,1)}, u32[]{:S(2)}, u32[]{:S(2)}) async-start(bf16[16,2,16384]{2,1,0:T(2,128)(2,1)} %reshape.260), calls=%async_computation.3 | async-start | bytes 2097152 | tf_op jit(solution)/shard_map/all_to_all | solution.py:128
  149.3 8.2 %collective-permute-start = (bf16[2,64,256]{2,1,0:T(8,128)(2,1)S(1)}, bf16[2,64,256]{2,1,0:T(8,128)(2,1)S(1)}, u32[]{:S(2)}, u32[]{:S(2)}) collective-permute-start(bf16[2,64,256]{2,1,0:T(8,128)(2,1)S(1)} %slice_bitcast_fusion.1), channel_id=1, source_target_pairs={{0,1},{1,2},{2,3},{4,5},{5,6},{6,7},{8,9},{9,10},{10,11},{12,13},{... | collective-permute-start | bytes 196616 | tf_op jit(solution)/shard_map/ppermute | solution.py:14
  158.2 7.8 %collective-permute-done = bf16[2,64,256]{2,1,0:T(8,128)(2,1)S(1)} collective-permute-done((bf16[2,64,256]{2,1,0:T(8,128)(2,1)S(1)}, bf16[2,64,256]{2,1,0:T(8,128)(2,1)S(1)}, u32[]{:S(2)}, u32[]{:S(2)}) %collective-permute-start) | collective-permute-done | bytes 65568 | tf_op jit(solution)/shard_map/ppermute | solution.py:14
  172.2 3.8 reshape.261
  176.0 3.1 convert_multiply_fusion
  179.0 71.3 %scatter_fusion.5 = f32[8,64,256]{1,0,2:T(8,128)S(1)} fusion(f32[8,64,256]{1,0,2:T(8,128)S(1)} %copy.92, s32[1024]{0:T(1024)S(1)} %reshape.131, f32[1024,8,64]{2,1,0:T(8,128)} %bitcast.272), kind=kCustom, calls=%fused_computation.9 | custom fusion | flops 524288 | bytes 6295552 | tf_op jit(solution)/shard_map/scatter-add | solution.py:74
  252.6 7.6 %gather_fusion = bf16[1024,8,64]{2,1,0:T(8,128)(2,1)} fusion(bf16[8,64,256]{1,0,2:T(8,128)(2,1)S(1)} %copy.63, s32[1024]{0:T(1024)S(1)} %broadcast_clamp_fusion), kind=kCustom, calls=%fused_computation | custom fusion | bytes 2101248 | tf_op jit(solution)/shard_map/gather | solution.py:23
  260.2 4.9 fusion.76
  267.3 7.9 %all-to-all-start = ((bf16[16,2,16384]{2,1,0:T(2,128)(2,1)}), bf16[16,2,16384]{2,1,0:T(2,128)(2,1)S(1)}, u32[]{:S(2)}, u32[]{:S(2)}) async-start(bf16[16,2,16384]{2,1,0:T(2,128)(2,1)} %reshape.254), calls=%async_computation | async-start | bytes 2097152 | tf_op jit(solution)/shard_map/all_to_all | solution.py:107
  276.1 21.2 %all-to-all-done = bf16[16,2,16384]{2,1,0:T(2,128)(2,1)S(1)} async-done(((bf16[16,2,16384]{2,1,0:T(2,128)(2,1)}), bf16[16,2,16384]{2,1,0:T(2,128)(2,1)S(1)}, u32[]{:S(2)}, u32[]{:S(2)}) %all-to-all-start) | async-done | bytes 1048608 | tf_op jit(solution)/shard_map/all_to_all | solution.py:107
  297.4 2.3 reshape.255
  299.7 3.4 pad_maximum_fusion
  303.1 3.4 copy.65
  306.5 2.3 gather_fusion.1
  309.9 3.3 gather_fusion.2
  313.3 4.8 fusion.77
  318.0 4.7 reshape.256
  322.7 7.9 %all-to-all-start.1 = ((bf16[16,2,16384]{2,1,0:T(2,128)(2,1)}), bf16[16,2,16384]{2,1,0:T(2,128)(2,1)S(1)}, u32[]{:S(2)}, u32[]{:S(2)}) async-start(bf16[16,2,16384]{2,1,0:T(2,128)(2,1)} %reshape.256), calls=%async_computation.1 | async-start | bytes 2097152 | tf_op jit(solution)/shard_map/all_to_all | solution.py:110
  336.4 4.1 collective-permute-start.1
  340.7 236.7 %all-reduce.3.cloned.1.call-done = f32[2,128,64]{1,2,0:T(8,128)} async-done(((f32[2,128,64]{1,2,0:T(8,128)}), f32[2,128,64]{1,2,0:T(8,128)}) %all-reduce.3.cloned.1.call-update) | async-done | bytes 65552 | tf_op jit(solution)/shard_map/psum | solution.py:178
  582.9 2.3 reshape.257
  585.3 3.4 pad_maximum_fusion.1
  588.7 3.4 copy.71
  592.1 2.3 gather_fusion.3
  597.1 75.0 %all-reduce = (f32[128]{0:T(128)S(1)}, f32[3,64,64]{1,2,0:T(8,128)S(1)}, f32[64]{0:T(128)S(1)}) all-reduce(f32[128]{0:T(128)S(1)} %convert_reduce_fusion, f32[3,64,64]{1,2,0:T(8,128)S(1)} %pad_maximum_fusion.6, f32[64]{0:T(128)S(1)} %convert_reduce_fusion.1), channel_id=1, replica_groups=mesh['dp'=4,'space'=16,'tm'=4] {'dp','space','tm'}, use_global_device_ids=true, to_apply=%region_8.0 | all-reduce | flops 12480 | bytes 99840 | tf_op jit(solution)/shard_map/psum | solution.py:178
  (135 shorter events, 50.1 us)
Async XLA Ops:
  17.3 11.6 %copy-start.1 = (bf16[2,8,128,128]{3,2,1,0:T(8,128)(2,1)S(1)}, bf16[2,8,128,128]{3,2,1,0:T(8,128)(2,1)}, u32[]{:S(2)}) copy-start(bf16[2,8,128,128]{3,2,1,0:T(8,128)(2,1)} %param.16) | copy-start | bytes 1572868
  19.6 31.6 %all-to-all-start.2 = ((bf16[16,2,16384]{2,1,0:T(2,128)(2,1)}), bf16[16,2,16384]{2,1,0:T(2,128)(2,1)}, u32[]{:S(2)}, u32[]{:S(2)}) async-start(bf16[16,2,16384]{2,1,0:T(2,128)(2,1)} %reshape.258), calls=%async_computation.2 | async-start | bytes 2097152 | tf_op jit(solution)/shard_map/all_to_all | solution.py:117
  29.7 1.9 copy-start
  29.7 1.9 copy-start.19
  31.6 0.8 copy-start.24
  129.3 1.0 copy-start.2
  139.3 10.0 %copy-start.12 = (bf16[1,8,64,256]{3,2,1,0:T(8,128)(2,1)S(1)}, bf16[1,8,64,256]{3,2,1,0:T(8,128)(2,1)}, u32[]{:S(2)}) copy-start(bf16[1,8,64,256]{3,2,1,0:T(8,128)(2,1)} %param.10) | copy-start | bytes 786436
  141.6 16.2 %copy-start.21 = (bf16[2,128,64]{1,2,0:T(8,128)(2,1)S(1)}, bf16[2,128,64]{1,2,0:T(8,128)(2,1)}, u32[]{:S(2)}) copy-start(bf16[2,128,64]{1,2,0:T(8,128)(2,1)} %param.12) | copy-start | bytes 98308
  141.6 24.4 %copy-start.26 = (f32[128]{0:T(128)S(1)}, f32[128]{0:T(128)}, u32[]{:S(2)}) copy-start(f32[128]{0:T(128)} %param.13) | copy-start | bytes 1540
  141.6 30.6 %all-to-all-start.3 = ((bf16[16,2,16384]{2,1,0:T(2,128)(2,1)}), bf16[16,2,16384]{2,1,0:T(2,128)(2,1)}, u32[]{:S(2)}, u32[]{:S(2)}) async-start(bf16[16,2,16384]{2,1,0:T(2,128)(2,1)} %reshape.260), calls=%async_computation.3 | async-start | bytes 2097152 | tf_op jit(solution)/shard_map/all_to_all | solution.py:128
  149.3 16.6 %collective-permute-start = (bf16[2,64,256]{2,1,0:T(8,128)(2,1)S(1)}, bf16[2,64,256]{2,1,0:T(8,128)(2,1)S(1)}, u32[]{:S(2)}, u32[]{:S(2)}) collective-permute-start(bf16[2,64,256]{2,1,0:T(8,128)(2,1)S(1)} %slice_bitcast_fusion.1), channel_id=1, source_target_pairs={{0,1},{1,2},{2,3},{4,5},{5,6},{6,7},{8,9},{9,10},{10,11},{12,13},{... | collective-permute-start | bytes 196616 | tf_op jit(solution)/shard_map/ppermute | solution.py:14
  157.8 8.2 %copy-start.17 = (bf16[6,64,256]{2,1,0:T(8,128)(2,1)}, bf16[6,64,256]{2,1,0:T(8,128)(2,1)S(1)}, u32[]{:S(2)}) copy-start(bf16[6,64,256]{2,1,0:T(8,128)(2,1)S(1)} %slice_bitcast_fusion) | copy-start | bytes 589828
  250.3 1.2 copy-start.11
  251.9 23.9 %copy-start.5 = (bf16[8,64,256]{2,1,0:T(8,128)(2,1)}, bf16[8,64,256]{2,1,0:T(8,128)(2,1)S(1)}, u32[]{:S(2)}) copy-start(bf16[8,64,256]{2,1,0:T(8,128)(2,1)S(1)} %get-tuple-element.27) | copy-start | bytes 786436
  251.9 23.9 %copy-start.7 = (bf16[8,64,256]{2,1,0:T(8,128)(2,1)}, bf16[8,64,256]{2,1,0:T(8,128)(2,1)S(1)}, u32[]{:S(2)}) copy-start(bf16[8,64,256]{2,1,0:T(8,128)(2,1)S(1)} %get-tuple-element.28) | copy-start | bytes 786436
  265.1 10.2 %copy-start.22 = (s32[2,8]{1,0:T(2,128)S(1)}, s32[2,8]{1,0:T(2,128)}, u32[]{:S(2)}) copy-start(s32[2,8]{1,0:T(2,128)} %param.17) | copy-start | bytes 196
  267.3 8.2 %copy-start.18 = (bf16[6,64,256]{2,1,0:T(8,128)(2,1)S(1)}, bf16[6,64,256]{2,1,0:T(8,128)(2,1)}, u32[]{:S(2)}) copy-start(bf16[6,64,256]{2,1,0:T(8,128)(2,1)} %copy-done.17) | copy-start | bytes 589828
  267.3 8.5 %copy-start.13 = (bf16[1,8,64,256]{3,2,1,0:T(8,128)(2,1)S(1)}, bf16[1,8,64,256]{3,2,1,0:T(8,128)(2,1)}, u32[]{:S(2)}) copy-start(bf16[1,8,64,256]{3,2,1,0:T(8,128)(2,1)} %param.10) | copy-start | bytes 786436
  267.3 30.0 %all-to-all-start = ((bf16[16,2,16384]{2,1,0:T(2,128)(2,1)}), bf16[16,2,16384]{2,1,0:T(2,128)(2,1)S(1)}, u32[]{:S(2)}, u32[]{:S(2)}) async-start(bf16[16,2,16384]{2,1,0:T(2,128)(2,1)} %reshape.254), calls=%async_computation | async-start | bytes 2097152 | tf_op jit(solution)/shard_map/all_to_all | solution.py:107
  306.5 2.3 copy-start.3
  318.0 13.4 %copy-start.6 = (bf16[8,64,256]{2,1,0:T(8,128)(2,1)S(1)}, bf16[8,64,256]{2,1,0:T(8,128)(2,1)}, u32[]{:S(2)}) copy-start(bf16[8,64,256]{2,1,0:T(8,128)(2,1)} %copy-done.5) | copy-start | bytes 786436
  318.0 13.4 %copy-start.8 = (bf16[8,64,256]{2,1,0:T(8,128)(2,1)S(1)}, bf16[8,64,256]{2,1,0:T(8,128)(2,1)}, u32[]{:S(2)}) copy-start(bf16[8,64,256]{2,1,0:T(8,128)(2,1)} %copy-done.7) | copy-start | bytes 786436
  322.7 8.7 %copy-start.10 = (bf16[8,64,256]{2,1,0:T(8,128)(2,1)S(1)}, bf16[8,64,256]{2,1,0:T(8,128)(2,1)}, u32[]{:S(2)}) copy-start(bf16[8,64,256]{2,1,0:T(8,128)(2,1)} %copy-done.9) | copy-start | bytes 786436
  322.7 11.3 %copy-start.14 = (bf16[1,8,64,256]{3,2,1,0:T(8,128)(2,1)S(1)}, bf16[1,8,64,256]{3,2,1,0:T(8,128)(2,1)}, u32[]{:S(2)}) copy-start(bf16[1,8,64,256]{3,2,1,0:T(8,128)(2,1)} %param.10) | copy-start | bytes 786436
  322.7 11.3 %copy-start.25 = (f32[64]{0:T(128)S(1)}, f32[64]{0:T(128)}, u32[]{:S(2)}) copy-start(f32[64]{0:T(128)} %param.15) | copy-start | bytes 772
  322.7 260.2 %all-to-all-start.1 = ((bf16[16,2,16384]{2,1,0:T(2,128)(2,1)}), bf16[16,2,16384]{2,1,0:T(2,128)(2,1)S(1)}, u32[]{:S(2)}, u32[]{:S(2)}) async-start(bf16[16,2,16384]{2,1,0:T(2,128)(2,1)} %reshape.256), calls=%async_computation.1 | async-start | bytes 2097152 | tf_op jit(solution)/shard_map/all_to_all | solution.py:110
  330.7 246.8 %all-reduce.3.cloned.1.call-start = ((), (), s32[]{:S(2)}) async-start(), calls=%async_computation.4 | async-start | bytes 131072 | tf_op jit(solution)/shard_map/psum | solution.py:178
  335.7 245.5 %copy-start.16 = (f32[8,64,256]{2,1,0:T(8,128)S(1)}, f32[8,64,256]{2,1,0:T(8,128)}, u32[]{:S(2)}) copy-start(f32[8,64,256]{2,1,0:T(8,128)} %fusion.4) | copy-start | bytes 1572868
  336.4 242.5 %collective-permute-start.1 = (bf16[2,128,256]{2,1,0:T(8,128)(2,1)}, bf16[2,128,256]{2,1,0:T(8,128)(2,1)}, u32[]{:S(2)}, u32[]{:S(2)}) collective-permute-start(bf16[2,128,256]{2,1,0:T(8,128)(2,1)} %fusion.50), channel_id=1, source_target_pairs={{1,0},{2,1},{3,2},{5,4},{6,5},{7,6},{9,8},{10,9},{11,10},{13,12},{... | collective-permute-start | bytes 393224 | tf_op jit(solution)/shard_map/ppermute | solution.py:14
  592.1 2.3 copy-start.4
  594.4 1.0 copy-start.15
  594.4 2.7 copy-start.20
  (2 other events, 1.4 us)
Sparse Core Ops, SparseCore 0:
  337.6 239.8 all-reduce.2
where the time goes:
time: 688 us; the launch traced here: 681 us
  waiting for transfers between devices  286 us (42%)
  other arithmetic  183 us (27%)
  blocking collectives  75 us (11%)
  local copies, waits for them, and re-layouts  58.8 us (9%)
  starting transfers between devices  45.1 us (7%)
  matrix products  18.1 us (3%)
  between operations  14.7 us (2%)
    psum x1, waiting for transfers between devices, body(): lax.psum((grad_conv_w, grad_conv_b, grad_mix_w, grad_mix_b), ('dp', 'spac...  237 us
    scatter-add x2, other arithmetic, back_finish(): total.at[:, :, send_rows[0]].add(returned * live_slots.astype(jnp.float32))  143 us
    psum x1, blocking collectives, body(): lax.psum((grad_conv_w, grad_conv_b, grad_mix_w, grad_mix_b), ('dp', 'spac...  75 us
    unnamed x63, local copies, waits for them, and re-layouts  26.4 us
    all_to_all x1, waiting for transfers between devices, body(): lax.all_to_all(packed_one, 'space', split_axis=2, concat_axis=2, tiled=True)  21.2 us
    all_to_all x1, waiting for transfers between devices, body(): lax.all_to_all(back_start(back_two, adj_tiles, tile_cols, send_rows), 'sp...  18.7 us
  transfers between devices with their start and end apart: 7, of which 5 were waited for; matrix products, arithmetic and copies ran while one was open for 3% of the time, Pallas kernels for 0%

commit v1 on v0

v1 whole, which is shorter than its diff:
```python
import functools
import math

import jax
import jax.numpy as jnp
from jax import lax
from jax.experimental import pallas as pl
from jax.experimental.pallas import tpu as pltpu
from jax.sharding import PartitionSpec as P

MESH = pl.DeviceIdType.MESH
F32 = jnp.float32
BF16 = jnp.bfloat16


def nn(a, b):
    return jnp.dot(a, b, preferred_element_type=F32)


def nt(a, b):
    return lax.dot_general(a, b, (((1,), (1,)), ((), ())), preferred_element_type=F32)


def kernel(
    dims,
    x_ref, g_ref, convw_ref, convb_ref, mixw_ref, mixb_ref, adj_ref, cols_ref, idx_ref,
    out_ref, gin_ref, gcw_ref, gcb_ref, gmw_ref, gmb_ref,
    xb, bpb, xt, gt, wt, wtt, mcat, gm, gmt, dm, dmt,
    b2, b1, b1base, b0base, filt, gate, hid, hop1, hop2, bp,
    sq1, sf1, sq2, sf2, rq1, rf1, rq2, rf2,
    pay_c, pay_m, ra_c, ra_m, rb_c, rb_m, fin_c, fin_m, sum_c, sum_m,
    ssem, rsem, assem, arsem, nsem,
):
    n_space, n_dp, n_tm, scale = dims
    me = lax.axis_index("space")
    tm = lax.axis_index("tm")
    dp = lax.axis_index("dp")
    grp = dp * n_tm + tm
    n_grp = n_dp * n_tm

    def space_dev(k):
        return {"space": k}

    def grp_dev(k):
        return {"dp": lax.div(k, n_tm), "tm": lax.rem(k, n_tm)}

    barrier = pltpu.get_barrier_semaphore()

    @pl.loop(1, n_space)
    def _(off):
        pl.semaphore_signal(
            barrier, inc=1, device_id=space_dev(lax.rem(me + off, n_space)), device_id_type=MESH
        )

    @pl.loop(1, n_grp)
    def _(off):
        pl.semaphore_signal(
            barrier, inc=1, device_id=grp_dev(lax.rem(grp + off, n_grp)), device_id_type=MESH
        )

    def exchange(mine, count, dev, src, dst, ss, rs):
        def copy(tgt, frm):
            return pltpu.make_async_remote_copy(
                src_ref=src(tgt), dst_ref=dst(frm), send_sem=ss.at[tgt], recv_sem=rs.at[frm],
                device_id=dev(tgt), device_id_type=MESH,
            )

        def start():
            @pl.loop(1, count)
            def _(off):
                copy(lax.rem(mine + off, count), mine).start()

        def wait_recv():
            @pl.loop(1, count)
            def _(off):
                copy(lax.rem(mine + off, count), lax.rem(mine + (count - off), count)).wait_recv()

        def wait_send():
            @pl.loop(1, count)
            def _(off):
                copy(lax.rem(mine + off, count), mine).wait_send()

        return start, wait_recv, wait_send

    slots = 64

    def rows(ref, size):
        def at(k):
            return ref.at[pl.ds(pl.multiple_of(k * size, size), size), :]

        return at

    def halo(i, send, recv):
        return exchange(
            me, n_space, space_dev, rows(send, slots), rows(recv, slots), ssem.at[i], rsem.at[i]
        )

    q1_start, q1_recv, q1_sent = halo(0, sq1, rq1)
    f1_start, f1_recv, f1_sent = halo(1, sf1, rf1)
    q2_start, q2_recv, q2_sent = halo(2, sq2, rq2)
    f2_start, f2_recv, f2_sent = halo(3, sf2, rf2)

    def next_copy():
        return pltpu.make_async_remote_copy(
            src_ref=x_ref.at[pl.ds(384, 128), :], dst_ref=xb, send_sem=nsem.at[0], recv_sem=nsem.at[1],
            device_id={"tm": lax.rem(tm + 1, n_tm)}, device_id_type=MESH,
        )

    def back_copy():
        return pltpu.make_async_remote_copy(
            src_ref=bp.at[:, pl.ds(0, 256)], dst_ref=bpb, send_sem=nsem.at[2], recv_sem=nsem.at[3],
            device_id={"tm": lax.rem(tm + n_tm - 1, n_tm)}, device_id_type=MESH,
        )

    pl.semaphore_wait(barrier, n_space - 1 + n_grp - 1)

    @pl.when(tm < n_tm - 1)
    def _():
        next_copy().start()

    @pl.when(tm == 0)
    def _():
        xb[...] = jnp.zeros_like(xb)

    @pl.when(tm == n_tm - 1)
    def _():
        bpb[...] = jnp.zeros_like(bpb)

    own_slots = pl.ds(pl.multiple_of(me * slots, slots), slots)
    for ref in (rq1, rf1, rq2, rf2):
        ref[own_slots, :] = jnp.zeros((slots, 512), BF16)

    zero = jnp.zeros((64, 64), F32)

    def pair(w):
        w = w.astype(F32)
        top = jnp.concatenate([w, zero], 1)
        low = jnp.concatenate([zero, w], 1)
        return jnp.concatenate([top, low], 0)

    for k in range(3):
        mcat[:, 128 * k : 128 * (k + 1)] = pair(mixw_ref[k]).astype(BF16)
    for half in range(2):
        for tap in range(2):
            block = pair(convw_ref[tap, 64 * half : 64 * (half + 1), :])
            wt[128 * half : 128 * (half + 1), 128 * tap : 128 * (tap + 1)] = block.astype(BF16)
            wtt[128 * tap : 128 * (tap + 1), 128 * half : 128 * (half + 1)] = block.T.astype(BF16)

    for r in range(2):
        for b in range(10):
            total = None
            for k in range(4):
                slot = k if b < 2 else 4 + k
                hit = (cols_ref[r, slot] == b).astype(F32)
                term = adj_ref[r, slot].astype(F32) * hit
                total = term if total is None else total + term
            dm[128 * r : 128 * (r + 1), 128 * b : 128 * (b + 1)] = total.astype(BF16)
            dmt[128 * b : 128 * (b + 1), 128 * r : 128 * (r + 1)] = total.T.astype(BF16)

    for p in range(4):
        lanes = slice(128 * p, 128 * (p + 1))
        gt[:, lanes] = g_ref[lanes, :].T
        terms = nn(gt[:, lanes], mcat[...])
        b0base[:, lanes] = terms[:, :128]
        b1base[:, lanes] = terms[:, 128:256]
        b2[:, lanes] = terms[:, 256:].astype(BF16)

    def halo_sums(src, dst):
        @pl.loop(0, 4)
        def _(m):
            at = pl.multiple_of(m * 256, 256)
            dst[pl.ds(at, 256), :] = nn(dmt[pl.ds(at + 256, 256), :], src[...]).astype(BF16)

    def pack(src, dst):
        @pl.loop(0, 4)
        def _(m):
            at = pl.multiple_of(m * 256, 256)
            dst[pl.ds(at, 256), :] = nn(gmt[pl.ds(at, 256), :], src[...]).astype(BF16)

    halo_sums(b2, sq1)
    q1_start()

    for m in range(4):
        lanes = slice(256 * m, 256 * (m + 1))
        sensor = lax.broadcasted_iota(jnp.int32, (256, 256), 0)
        block = (sensor == idx_ref[0:1, lanes]).astype(F32)
        gm[:, lanes] = block.astype(BF16)
        gmt[lanes, :] = block.T.astype(BF16)

    for p in range(4):
        xt[:, 128 * (p + 1) : 128 * (p + 2)] = x_ref[128 * p : 128 * (p + 1), :].T

    @pl.when(tm > 0)
    def _():
        next_copy().wait_recv()

    xt[:, 0:128] = xb[...].T
    b = convb_ref[...]
    bias = jnp.concatenate([b[:, :64], b[:, :64], b[:, 64:], b[:, 64:]], 1)
    for p in range(4):
        lanes = slice(128 * p, 128 * (p + 1))
        pre = nt(xt[:, 128 * p : 128 * p + 256], wt[...]) + bias
        f = jnp.tanh(pre[:, :128])
        s = jax.nn.sigmoid(pre[:, 128:])
        filt[:, lanes] = f
        gate[:, lanes] = s
        hid[:, lanes] = (f * s).astype(BF16)
    pack(hid, sf1)
    f1_start()

    q1_recv()
    for m in range(2):
        at = slice(128 * m, 128 * (m + 1))
        b1[at, :] = (b1base[at, :] + nn(dmt[at, :], b2[...]) + nn(gm[at, :], rq1[...])).astype(BF16)
    halo_sums(b1, sq2)
    q2_start()

    f1_recv()
    for m in range(2):
        at = slice(128 * m, 128 * (m + 1))
        hop1[at, :] = (nn(dm[at, :256], hid[...]) + nn(dm[at, 256:], rf1[...])).astype(BF16)
    pack(hop1, sf2)
    f2_start()

    acc0 = acc1 = None
    for p in range(4):
        lanes = slice(128 * p, 128 * (p + 1))
        a0 = nn(g_ref[lanes, :], hid[:, lanes])
        a1 = nn(g_ref[lanes, :], hop1[:, lanes])
        acc0 = a0 if acc0 is None else acc0 + a0
        acc1 = a1 if acc1 is None else acc1 + a1
    low_lanes = lax.broadcasted_iota(jnp.int32, (64, 128), 1) < 64

    def diag_low(a):
        return a[:64] + pltpu.roll(a[64:], 64, 1)

    def diag_high(a):
        return pltpu.roll(a[:64], 64, 1) + a[64:]

    pay_m[0:64, :] = jnp.where(low_lanes, diag_low(acc0), diag_high(acc1))
    gsum = jnp.zeros((1, 128), F32)
    for p in range(4):
        gsum = gsum + jnp.sum(gt[:, 128 * p : 128 * (p + 1)].astype(F32), axis=0, keepdims=True)

    q2_recv()
    bsum = jnp.zeros((1, 256), F32)
    for p in range(4):
        lanes = slice(128 * p, 128 * (p + 1))
        bh = b0base[:, lanes] + nn(dmt[:256, :], b1[:, lanes]) + nn(gm[...], rq2[:, lanes])
        f = filt[:, lanes]
        s = gate[:, lanes]
        gf = (bh * (1.0 - f * f) * s).astype(BF16)
        gg = (bh * f * s * (1.0 - s)).astype(BF16)
        bp[:, 256 * p : 256 * p + 128] = gf
        bp[:, 256 * p + 128 : 256 * (p + 1)] = gg
        if p == 0:
            @pl.when(tm > 0)
            def _():
                back_copy().start()
        bsum = bsum + jnp.concatenate(
            [
                jnp.sum(gf.astype(F32), axis=0, keepdims=True),
                jnp.sum(gg.astype(F32), axis=0, keepdims=True),
            ],
            1,
        )
    acc_prev = nn(xb[...], bp[:, :256])
    acc_cur = nn(x_ref[0:128, :], bp[:, :256])
    for p in range(1, 4):
        lanes = slice(128 * p, 128 * (p + 1))
        wide = slice(256 * p, 256 * (p + 1))
        acc_prev = acc_prev + nn(x_ref[128 * (p - 1) : 128 * p, :], bp[:, wide])
        acc_cur = acc_cur + nn(x_ref[lanes, :], bp[:, wide])
    for tap, acc in ((0, acc_prev), (1, acc_cur)):
        pay_c[64 * tap : 64 * (tap + 1), :] = jnp.where(
            low_lanes, diag_low(acc[:, :128]), diag_high(acc[:, 128:])
        )

    def reduce_calls(i, pay, ra, rb, fin, part):
        chunk = 8
        s1 = exchange(
            me, n_space, space_dev, rows(pay, chunk), rows(ra, chunk), assem.at[3 * i], arsem.at[3 * i]
        )
        s2 = exchange(
            grp, n_grp, grp_dev, lambda k: part.at[0:8, :], rows(rb, chunk),
            assem.at[3 * i + 1], arsem.at[3 * i + 1],
        )
        s3 = exchange(
            me, n_space, space_dev, lambda k: part.at[8:16, :], rows(fin, chunk),
            assem.at[3 * i + 2], arsem.at[3 * i + 2],
        )
        mine = pl.ds(pl.multiple_of(me * chunk, chunk), chunk)
        ours = pl.ds(pl.multiple_of(grp * chunk, chunk), chunk)

        def first():
            ra[mine, :] = pay[mine, :]
            s1[0]()

        def second():
            s1[1]()
            total = ra[0:8, :]
            for k in range(1, n_space):
                total = total + ra[8 * k : 8 * k + 8, :]
            part[0:8, :] = total
            rb[ours, :] = total
            s2[0]()

        def third():
            s2[1]()
            total = rb[0:8, :]
            for k in range(1, n_grp):
                total = total + rb[8 * k : 8 * k + 8, :]
            total = total * scale
            part[8:16, :] = total
            fin[mine, :] = total
            s3[0]()

        def last():
            s3[1]()

        def sent():
            for s in (s1, s2, s3):
                s[2]()

        return first, second, third, last, sent

    c_first, c_second, c_third, c_last, c_sent = reduce_calls(0, pay_c, ra_c, rb_c, fin_c, sum_c)
    m_first, m_second, m_third, m_last, m_sent = reduce_calls(1, pay_m, ra_m, rb_m, fin_m, sum_m)
    c_first()

    def grad_in(p, nxt):
        lanes = slice(128 * p, 128 * (p + 1))
        here = nt(wtt[128:, :], bp[:, 256 * p : 256 * (p + 1)])
        gin_ref[lanes, :] = (g_ref[lanes, :].astype(F32) + here + nt(wtt[:128, :], nxt)).astype(BF16)

    for p in range(3):
        grad_in(p, bp[:, 256 * (p + 1) : 256 * (p + 2)])

    @pl.when(tm < n_tm - 1)
    def _():
        back_copy().wait_recv()

    grad_in(3, bpb[...])
    c_second()

    f2_recv()
    acc2 = None
    for m in range(2):
        at = slice(128 * m, 128 * (m + 1))
        hop2[at, :] = (nn(dm[at, :256], hop1[...]) + nn(dm[at, 256:], rf2[...])).astype(BF16)
    for p in range(4):
        lanes = slice(128 * p, 128 * (p + 1))
        a2 = nn(g_ref[lanes, :], hop2[:, lanes])
        acc2 = a2 if acc2 is None else acc2 + a2
    row = lax.broadcasted_iota(jnp.int32, (64, 128), 0)
    f_sum = bsum[:, :128]
    g_sum = bsum[:, 128:]
    f_sum = f_sum + pltpu.roll(f_sum, 64, 1)
    g_sum = g_sum + pltpu.roll(g_sum, 64, 1)
    o_sum = gsum + pltpu.roll(gsum, 64, 1)
    extra = jnp.where(row == 0, f_sum, jnp.where(row == 1, g_sum, jnp.where(row == 2, o_sum, 0.0)))
    pay_m[64:128, :] = jnp.where(low_lanes, diag_low(acc2), extra)
    m_first()
    c_third()

    mb = mixb_ref[...]
    mb = jnp.concatenate([mb, mb], 1)
    mb = jnp.broadcast_to(mb, (128, 128)).T
    mb = jnp.concatenate([mb, mb], 1)

    def mixed(p):
        lanes = slice(128 * p, 128 * (p + 1))
        total = x_ref[lanes, :].astype(F32) + mb
        for k, field in enumerate((hid, hop1, hop2)):
            total = total + nt(mcat[:, 128 * k : 128 * (k + 1)], field[:, lanes])
        out_ref[lanes, :] = total.astype(BF16)

    mixed(0)
    mixed(1)
    m_second()
    mixed(2)
    mixed(3)
    c_last()
    for tap in range(2):
        gcw_ref[tap] = fin_c[64 * tap : 64 * (tap + 1), :].T
    m_third()
    for s in (q1_sent, f1_sent, q2_sent, f2_sent, c_sent):
        s()

    @pl.when(tm < n_tm - 1)
    def _():
        next_copy().wait_send()

    @pl.when(tm > 0)
    def _():
        back_copy().wait_send()

    m_last()
    gmw_ref[0] = fin_m[0:64, 0:64]
    gmw_ref[1] = pltpu.roll(fin_m[0:64, :], 64, 1)[:, 0:64]
    gmw_ref[2] = fin_m[64:128, 0:64]
    tail = fin_m[64:72, :]
    gcb_ref[...] = jnp.where(low_lanes[0:1], pltpu.roll(tail[0:1], 64, 1), tail[1:2])
    gmb_ref[...] = pltpu.roll(tail[2:3], 64, 1)[:, 0:64]
    m_sent()


def body(dims, inputs, grad_out, conv_w, conv_b, mix_w, mix_b, adj_tiles, tile_cols, send_rows, counts):
    x = inputs.reshape(512, 256)
    g = grad_out.reshape(512, 256)
    slot = lax.broadcasted_iota(jnp.int32, send_rows.shape[1:], 1)
    idx = jnp.where(slot < counts[0][:, None], send_rows[0], -1).reshape(1, -1)
    vmem = pl.BlockSpec(memory_space=pltpu.VMEM)
    smem = pl.BlockSpec(memory_space=pltpu.SMEM)
    n_space = dims[0]
    n_grp = dims[1] * dims[2]

    def bf(*shape):
        return pltpu.VMEM(shape, BF16)

    def fl(*shape):
        return pltpu.VMEM(shape, F32)

    scratch = [
        bf(128, 256), bf(256, 256), bf(256, 640), bf(256, 512), bf(256, 256), bf(256, 256), bf(128, 384),
        bf(256, 1024), bf(1024, 256), bf(256, 1280), bf(1280, 256),
        bf(256, 512), bf(256, 512), fl(256, 512), fl(256, 512), fl(256, 512), fl(256, 512),
        bf(256, 512), bf(256, 512), bf(256, 512), bf(256, 1024),
    ]
    scratch += [bf(1024, 512)] * 8
    scratch += [fl(128, 128)] * 8 + [fl(16, 128)] * 2
    scratch += [
        pltpu.SemaphoreType.DMA((4, n_space)), pltpu.SemaphoreType.DMA((4, n_space)),
        pltpu.SemaphoreType.DMA((6, n_grp)), pltpu.SemaphoreType.DMA((6, n_grp)),
        pltpu.SemaphoreType.DMA((4,)),
    ]
    outs = pl.pallas_call(
        functools.partial(kernel, dims),
        out_shape=(
            jax.ShapeDtypeStruct((512, 256), BF16),
            jax.ShapeDtypeStruct((512, 256), BF16),
            jax.ShapeDtypeStruct((2, 128, 64), F32),
            jax.ShapeDtypeStruct((1, 128), F32),
            jax.ShapeDtypeStruct((3, 64, 64), F32),
            jax.ShapeDtypeStruct((1, 64), F32),
        ),
        in_specs=[vmem] * 7 + [smem, vmem],
        out_specs=(vmem,) * 6,
        scratch_shapes=scratch,
        compiler_params=pltpu.CompilerParams(
            collective_id=0, has_side_effects=True, vmem_limit_bytes=48 * 2**20
        ),
    )(x, g, conv_w, conv_b.reshape(1, 128), mix_w, mix_b.reshape(1, 64), adj_tiles, tile_cols, idx)
    out, gin, gcw, gcb, gmw, gmb = outs
    return (
        out.reshape(inputs.shape),
        gin.reshape(inputs.shape),
        gcw,
        gcb.reshape(128),
        gmw,
        gmb.reshape(64),
    )


def solution(mesh):
    in_specs = (
        P("dp", "tm", None, "space"),
        P("dp", "tm", None, "space"),
        P(),
        P(),
        P(),
        P(),
        P("space", None, None, None),
        P("space", None),
        P("space", None, None),
        P("space", None),
    )
    out_specs = (P("dp", "tm", None, "space"), P("dp", "tm", None, "space"), P(), P(), P(), P())
    cells = 512 * 256 // 64 * mesh.shape["dp"] * mesh.shape["space"] * mesh.shape["tm"]
    dims = (mesh.shape["space"], mesh.shape["dp"], mesh.shape["tm"], 1.0 / math.sqrt(cells))
    return jax.shard_map(
        functools.partial(body, dims), mesh=mesh, in_specs=in_specs, out_specs=out_specs, check_vma=False
    )
```

time: 688 us -> 141 us (0.20); the launches traced: 681 us -> 141 us
  waiting for transfers between devices: 286 us -> 0 us
  other arithmetic: 183 us -> 0.75 us
  Pallas kernels: 0 us -> 132 us
  blocking collectives: 75 us -> 0 us
  local copies, waits for them, and re-layouts: 58.8 us -> 7.66 us
  starting transfers between devices: 45.1 us -> 0 us
  matrix products: 18.1 us -> 0 us
  between operations: 14.7 us -> 0.72 us
    psum x1 -> x0, waiting for transfers between devices: 237 us -> none  [body(): lax.psum((grad_conv_w, grad_conv_b, grad_mix_w, grad_mix_b), ('dp', 'spac...]
    scatter-add x6 -> x0, other arithmetic: 153 us -> none  [the longest x2 143 us: back_finish(): total.at[:, :, send_rows[0]].add(returned * live_slots.astype(jnp.float32))]
    pallas_call x0 -> x1, Pallas kernels: none -> 132 us  [body(): pl.pallas_call(functools.partial(kernel, dims), out_shape=(jax.ShapeDtype...]
    psum x1 -> x0, blocking collectives: 75 us -> none  [body(): lax.psum((grad_conv_w, grad_conv_b, grad_mix_w, grad_mix_b), ('dp', 'spac...]
    all_to_all x4 -> x0, waiting for transfers between devices: 41.5 us -> none  [the longest x1 21.2 us: body(): lax.all_to_all(packed_one, 'space', split_axis=2, concat_axis=2, tiled=True)]
    all_to_all x4 -> x0, starting transfers between devices: 32.8 us -> none  [the longest x1 9.25 us: body(): lax.all_to_all(back_start(back_two, adj_tiles, tile_cols, send_rows), 'sp...]
    unnamed x63 -> x25, local copies, waits for them, and re-layouts: 26.4 us -> 7.5 us
    dot_general x21 -> x0, matrix products: 18.1 us -> none  [the longest x3 5.09 us: body(): jnp.einsum('oc,tcn->ton', mix_w[index], fields[index], preferred_element_...]
  transfers between devices with their start and end apart: 7 -> 0, of which waited for: 5 -> 0; matrix products, arithmetic and copies ran while one was open for 3% -> 0% of each run, Pallas kernels for 0% -> 0%
where the time goes in v1:
time: 141 us
  Pallas kernels  132 us (94%)
  local copies, waits for them, and re-layouts  7.66 us (5%)
    pallas_call x1, Pallas kernels, body(): pl.pallas_call(functools.partial(kernel, dims), out_shape=(jax.ShapeDtype...  132 us
    unnamed x25, local copies, waits for them, and re-layouts  7.5 us

profile of v1, /device:TPU:1, one launch (start us, length us, event | category | flops | bytes accessed | tf_op | source)
XLA Modules:
  0.0 141.1 jit_solution(17061537294780351814)
XLA Ops:
  0.6 0.0 copy-start.8
  0.6 0.0 copy-start.7
  0.7 0.7 iota_compare_fusion
  1.4 0.1 lt.23
  1.5 0.0 copy-done.8
  1.5 0.1 squeeze.3
  1.6 0.0 copy-done.7
  1.6 0.0 copy-start.3
  1.6 0.0 copy-start.4
  1.6 0.0 copy-start.5
  1.6 0.0 copy-start.6
  1.6 0.1 copy.16.convw_ref
  1.8 0.6 copy-done.3
  2.4 0.0 copy-done.4
  2.4 0.0 copy-done.5
  2.4 0.0 copy-done.6
  2.4 0.0 copy-start
  2.4 1.0 copy-done
  3.4 0.0 copy-start.1
  3.4 0.9 copy-done.1
  4.4 0.0 copy-start.2
  4.4 0.9 copy-done.2
  5.3 132.0 %shard_map.145 = (bf16[512,256]{1,0:T(8,128)(2,1)S(1)}, bf16[512,256]{1,0:T(8,128)(2,1)S(1)}, f32[2,128,64]{2,1,0:T(8,128)S(1)}, f32[1,128]{1,0:T(1,128)S(1)}, f...) custom-call(bf16[512,256]{1,0:T(8,128)(2,1)S(1)} %bitcast.11, bf16[512,256]{1,0:T(8,128)(2,1)S(1)} %bitcast.12, ...), custom_call_target="tpu_custom_call" | custom-call | tf_op jit(solution)/shard_map/pallas_call | solution.py:437
  137.4 0.7 copy.17
  138.1 0.7 copy.23
  138.8 0.7 copy.24
  139.5 0.5 copy.25
  140.0 0.6 copy.26
  140.6 0.5 copy.27
  (1 shorter events, 0.0 us)
Async XLA Ops:
  0.6 0.9 copy-start.8
  0.6 0.9 copy-start.7
  1.6 0.8 copy-start.3
  1.6 0.8 copy-start.4
  1.6 0.8 copy-start.5
  1.6 0.8 copy-start.6
  2.4 1.0 copy-start
  3.4 0.9 copy-start.1
  4.4 0.9 copy-start.2

commit v2 on v1

v2 whole, which is shorter than its diff:
```python
import functools
import math

import jax
import jax.numpy as jnp
from jax import lax
from jax.experimental import pallas as pl
from jax.experimental.pallas import tpu as pltpu
from jax.sharding import PartitionSpec as P

MESH = pl.DeviceIdType.MESH
F32 = jnp.float32
BF16 = jnp.bfloat16
SLOTS = 64
CHUNK = 16


def nn(a, b):
    return jnp.dot(a, b, preferred_element_type=F32)


def nt(a, b):
    return lax.dot_general(a, b, (((1,), (1,)), ((), ())), preferred_element_type=F32)


def exchange(mine, count, dev, src, dst, ss, rs):
    def copy(tgt, frm):
        return pltpu.make_async_remote_copy(
            src_ref=src(tgt), dst_ref=dst(frm), send_sem=ss.at[tgt], recv_sem=rs.at[frm],
            device_id=dev(tgt), device_id_type=MESH,
        )

    def start():
        @pl.loop(1, count)
        def _(off):
            copy(lax.rem(mine + off, count), mine).start()

    def received():
        @pl.loop(1, count)
        def _(off):
            copy(lax.rem(mine + off, count), lax.rem(mine + (count - off), count)).wait_recv()

    def sent():
        @pl.loop(1, count)
        def _(off):
            copy(lax.rem(mine + off, count), mine).wait_send()

    return copy, start, received, sent


def rows(ref, size):
    return lambda k: ref.at[pl.ds(pl.multiple_of(k * size, size), size), :]


def kernel(
    dims,
    x_hbm, g_hbm, adj_hbm, convw_ref, convb_ref, mixw_ref, mixb_ref, cols_ref, idx_ref,
    out_ref, gin_ref, fin,
    x_ref, g_ref, adj_ref, xb, bpb, xt, gt, wt, wtt, mcat, mcatv, gm, gmt, dm, dmt, dlo, dlot,
    qg, qqg, filt, gate, hid, hidn, hop1, hop2, bp, part,
    sq1, sq2, sf1, sf2, rq1, rq2, rf1, rf2,
    pay, ra, rb, sums,
    ssem, rsem, assem, arsem, nsem, lsem,
):
    n_space, n_dp, n_tm, scale = dims
    me = lax.axis_index("space")
    tm = lax.axis_index("tm")
    dp = lax.axis_index("dp")
    grp = dp * n_tm + tm
    n_grp = n_dp * n_tm
    z = lax.div(me, 4)
    y = lax.rem(me, 4)

    def space_dev(k):
        return {"space": k}

    def grp_dev(k):
        return {"dp": lax.div(k, n_tm), "tm": lax.rem(k, n_tm)}

    loads = [
        pltpu.make_async_copy(src, dst, lsem.at[i])
        for i, (src, dst) in enumerate(((g_hbm, g_ref), (adj_hbm, adj_ref), (x_hbm, x_ref)))
    ]
    for load in loads:
        load.start()

    barrier = pltpu.get_barrier_semaphore()

    @pl.loop(1, n_space)
    def _(off):
        pl.semaphore_signal(
            barrier, inc=1, device_id=space_dev(lax.rem(me + off, n_space)), device_id_type=MESH
        )

    @pl.loop(1, n_grp)
    def _(off):
        pl.semaphore_signal(
            barrier, inc=1, device_id=grp_dev(lax.rem(grp + off, n_grp)), device_id_type=MESH
        )

    def halo(i, send, recv):
        return [
            exchange(
                me, n_space, space_dev, rows(send.at[h], SLOTS), rows(recv.at[h], SLOTS),
                ssem.at[2 * i + h], rsem.at[2 * i + h],
            )
            for h in range(2)
        ]

    q1 = halo(0, sq1, rq1)
    q2 = halo(1, sq2, rq2)
    f1 = halo(2, sf1, rf1)
    f2 = halo(3, sf2, rf2)

    def by_distance(step):
        far = 1 - lax.div(step, 2)
        odd = lax.rem(lax.div(step + 1, 2), 2)
        return 2 * lax.rem(lax.div(z, 2) + far, 2) + lax.rem(lax.rem(z, 2) + odd, 2)

    def spread(ex, matrix, field, buf, h, compute=True, send=True):
        copy = ex[h][0]
        lanes = slice(256 * h, 256 * (h + 1))

        @pl.loop(0, 4)
        def _(step):
            zz = by_distance(step)
            if compute:
                at = pl.ds(pl.multiple_of(zz * 256, 256), 256)
                buf[h, at, :] = nn(matrix[at, :], field[:, lanes]).astype(BF16)
            if send:
                @pl.loop(0, 4)
                def _(k):
                    tgt = zz * 4 + lax.rem(y + k, 4)

                    @pl.when(tgt != me)
                    def _():
                        copy(tgt, me).start()

    def next_copy():
        return pltpu.make_async_remote_copy(
            src_ref=x_ref.at[pl.ds(384, 128), :], dst_ref=xb, send_sem=nsem.at[0], recv_sem=nsem.at[1],
            device_id={"tm": lax.rem(tm + 1, n_tm)}, device_id_type=MESH,
        )

    def back_copy():
        return pltpu.make_async_remote_copy(
            src_ref=bp.at[:, pl.ds(0, 256)], dst_ref=bpb, send_sem=nsem.at[2], recv_sem=nsem.at[3],
            device_id={"tm": lax.rem(tm + n_tm - 1, n_tm)}, device_id_type=MESH,
        )

    def tile_sum(r, b):
        total = None
        for k in range(4):
            slot = k if b < 2 else 4 + k
            hit = (cols_ref[r, slot] == b).astype(F32)
            term = adj_ref[r, slot].astype(F32) * hit
            total = term if total is None else total + term
        return total

    loads[0].wait()
    for p in range(4):
        gt[:, 128 * p : 128 * (p + 1)] = g_ref[128 * p : 128 * (p + 1), :].T
    loads[1].wait()
    for b in range(2, 10):
        for r in range(2):
            block = tile_sum(r, b).astype(BF16)
            dm[128 * r : 128 * (r + 1), 128 * b : 128 * (b + 1)] = block
            dmt[128 * (b - 2) : 128 * (b - 1), 128 * r : 128 * (r + 1)] = block.T

    own_slots = pl.ds(pl.multiple_of(me * SLOTS, SLOTS), SLOTS)
    for ref in (rq1, rq2, rf1, rf2):
        for h in range(2):
            ref[h, own_slots, :] = jnp.zeros((SLOTS, 256), BF16)
    loads[2].wait()
    pl.semaphore_wait(barrier, n_space - 1 + n_grp - 1)

    for h in range(2):
        spread(q1, dmt, gt, sq1, h)

    @pl.when(tm < n_tm - 1)
    def _():
        next_copy().start()

    @pl.when(tm == 0)
    def _():
        xb[...] = jnp.zeros_like(xb)

    @pl.when(tm == n_tm - 1)
    def _():
        bpb[...] = jnp.zeros_like(bpb)

    for b in range(2):
        for r in range(2):
            total = tile_sum(r, b)
            high = total.astype(BF16)
            low = (total - high.astype(F32)).astype(BF16)
            here = slice(128 * r, 128 * (r + 1)), slice(128 * b, 128 * (b + 1))
            dm[here] = high
            dlo[here] = low
            dlot[128 * b : 128 * (b + 1), 128 * r : 128 * (r + 1)] = high.T
            dlot[128 * b : 128 * (b + 1), 256 + 128 * r : 256 + 128 * (r + 1)] = low.T

    for m in range(4):
        lanes = slice(256 * m, 256 * (m + 1))
        sensor = lax.broadcasted_iota(jnp.int32, (256, 256), 0)
        block = (sensor == idx_ref[0:1, lanes]).astype(F32).astype(BF16)
        gm[:, lanes] = block
        gmt[lanes, :] = block.T

    zero = jnp.zeros((64, 64), F32)

    def pair(w):
        w = w.astype(F32)
        return jnp.concatenate([jnp.concatenate([w, zero], 1), jnp.concatenate([zero, w], 1)], 0)

    for k in range(3):
        block = pair(mixw_ref[k]).astype(BF16)
        mcat[:, 128 * k : 128 * (k + 1)] = block
        mcatv[128 * k : 128 * (k + 1), :] = block
    for half in range(2):
        for tap in range(2):
            block = pair(convw_ref[tap, 64 * half : 64 * (half + 1), :]).astype(BF16)
            wt[128 * half : 128 * (half + 1), 128 * tap : 128 * (tap + 1)] = block
            wtt[128 * tap : 128 * (tap + 1), 128 * half : 128 * (half + 1)] = block.T

    for p in range(4):
        xt[:, 128 * (p + 1) : 128 * (p + 2)] = x_ref[128 * p : 128 * (p + 1), :].T

    @pl.when(tm > 0)
    def _():
        next_copy().wait_recv()

    xt[:, 0:128] = xb[...].T
    b = convb_ref[...]
    bias = jnp.concatenate([b[:, :64], b[:, :64], b[:, 64:], b[:, 64:]], 1)
    for p in range(4):
        lanes = slice(128 * p, 128 * (p + 1))
        pre = nt(xt[:, 128 * p : 128 * p + 256], wt[...]) + bias
        f = jnp.tanh(pre[:, :128])
        s = jax.nn.sigmoid(pre[:, 128:])
        filt[:, lanes] = f
        gate[:, lanes] = s
        hid[:, lanes] = (f * s).astype(BF16)

    for h in range(2):
        lanes = slice(256 * h, 256 * (h + 1))
        q1[h][2]()
        grad = gt[:, lanes]
        own = nn(dlot[:, :256], grad) + nn(dlot[:, 256:], grad)
        qg[:, lanes] = (own + nn(gm[...], rq1[h])).astype(BF16)
        spread(q2, dmt, qg, sq2, h)

    spread(f1, gmt, hid, sf1, 0)
    spread(f1, gmt, hid, sf1, 1, send=False)
    for p in range(4):
        lanes = slice(128 * p, 128 * (p + 1))
        hidn[lanes, :] = hid[:, lanes].T
    gsum = jnp.zeros((1, 128), F32)
    for p in range(4):
        gsum = gsum + jnp.sum(gt[:, 128 * p : 128 * (p + 1)].astype(F32), axis=0, keepdims=True)

    low_lanes = lax.broadcasted_iota(jnp.int32, (64, 128), 1) < 64

    def diag_low(a):
        return a[:64] + pltpu.roll(a[64:], 64, 1)

    def diag_high(a):
        return pltpu.roll(a[:64], 64, 1) + a[64:]

    bsum = jnp.zeros((1, 256), F32)
    accs = [None] * 5

    def add(i, term):
        accs[i] = term if accs[i] is None else accs[i] + term

    for h in range(2):
        lanes = slice(256 * h, 256 * (h + 1))
        q2[h][2]()
        grad = qg[:, lanes]
        own = nn(dlot[:, :256], grad) + nn(dlot[:, 256:], grad)
        qqg[:, lanes] = (own + nn(gm[...], rq2[h])).astype(BF16)
        for p in (2 * h, 2 * h + 1):
            lanes = slice(128 * p, 128 * (p + 1))
            three = (gt[:, lanes], qg[:, lanes], qqg[:, lanes])
            bh = nn(jnp.concatenate(three, 1), mcatv[...])
            f = filt[:, lanes]
            s = gate[:, lanes]
            gf = (bh * (1.0 - f * f) * s).astype(BF16)
            gg = (bh * f * s * (1.0 - s)).astype(BF16)
            bp[:, 256 * p : 256 * p + 128] = gf
            bp[:, 256 * p + 128 : 256 * (p + 1)] = gg
            if p == 0:
                @pl.when(tm > 0)
                def _():
                    back_copy().start()
            bsum = bsum + jnp.concatenate(
                [
                    jnp.sum(gf.astype(F32), axis=0, keepdims=True),
                    jnp.sum(gg.astype(F32), axis=0, keepdims=True),
                ],
                1,
            )
            for k in range(3):
                add(k, nn(hidn[lanes, :], three[k]))
            wide = bp[:, 256 * p : 256 * (p + 1)]
            add(3, nn(xb[...] if p == 0 else x_ref[128 * (p - 1) : 128 * p, :], wide))
            add(4, nn(x_ref[lanes, :], wide))
    row = lax.broadcasted_iota(jnp.int32, (64, 128), 0)
    f_sum = bsum[:, :128]
    g_sum = bsum[:, 128:]
    f_sum = f_sum + pltpu.roll(f_sum, 64, 1)
    g_sum = g_sum + pltpu.roll(g_sum, 64, 1)
    o_sum = gsum + pltpu.roll(gsum, 64, 1)
    extra = jnp.where(row == 0, f_sum, jnp.where(row == 1, g_sum, jnp.where(row == 2, o_sum, 0.0)))
    pay[0:64, :] = jnp.where(low_lanes, diag_low(accs[0]), diag_high(accs[1]))
    pay[64:128, :] = jnp.where(low_lanes, diag_low(accs[2]), extra)
    for tap in range(2):
        acc = accs[3 + tap]
        pay[128 + 64 * tap : 192 + 64 * tap, :] = jnp.where(
            low_lanes, diag_low(acc[:, :128]), diag_high(acc[:, 128:])
        )

    s1 = exchange(me, n_space, space_dev, rows(pay, CHUNK), rows(ra, CHUNK), assem.at[0], arsem.at[0])
    s2 = exchange(grp, n_grp, grp_dev, lambda k: sums.at[0], rows(rb, CHUNK), assem.at[1], arsem.at[1])
    s3 = exchange(me, n_space, space_dev, lambda k: sums.at[1], rows(fin, CHUNK), assem.at[2], arsem.at[2])
    mine = pl.ds(pl.multiple_of(me * CHUNK, CHUNK), CHUNK)
    ours = pl.ds(pl.multiple_of(grp * CHUNK, CHUNK), CHUNK)

    def total_of(ref, count):
        total = ref[0:CHUNK, :]
        for k in range(1, count):
            total = total + ref[CHUNK * k : CHUNK * (k + 1), :]
        return total

    ra[mine, :] = pay[mine, :]
    s1[1]()
    spread(f1, gmt, hid, sf1, 1, compute=False)

    def grad_in(p, nxt):
        lanes = slice(128 * p, 128 * (p + 1))
        here = nt(wtt[128:, :], bp[:, 256 * p : 256 * (p + 1)])
        gin_ref[lanes, :] = (g_ref[lanes, :].astype(F32) + here + nt(wtt[:128, :], nxt)).astype(BF16)

    mb = mixb_ref[...]
    mb = jnp.broadcast_to(jnp.concatenate([mb, mb], 1), (128, 128)).T
    mb = jnp.concatenate([mb, mb], 1)

    for p in range(3):
        grad_in(p, bp[:, 256 * (p + 1) : 256 * (p + 2)])

    s1[2]()
    total = total_of(ra, n_space)
    sums[0] = total
    rb[ours, :] = total
    s2[1]()

    def hop(dst, src, recv, h):
        lanes = slice(256 * h, 256 * (h + 1))
        field = src[:, lanes]
        own = nn(dm[:, :256], field) + nn(dlo[...], field)
        dst[:, lanes] = (own + nn(dm[:, 256:], recv[h])).astype(BF16)

    def mixed(p, last):
        lanes = slice(128 * p, 128 * (p + 1))
        if last:
            here = nt(mcat[:, 256:], hop2[:, lanes])
            out_ref[lanes, :] = (part[lanes, :] + here).astype(BF16)
        else:
            here = nt(mcat[:, :128], hid[:, lanes]) + nt(mcat[:, 128:256], hop1[:, lanes])
            part[lanes, :] = x_ref[lanes, :].astype(F32) + mb + here

    f1[0][2]()
    hop(hop1, hid, rf1, 0)
    spread(f2, gmt, hop1, sf2, 0)
    mixed(0, False)
    mixed(1, False)
    f1[1][2]()
    hop(hop1, hid, rf1, 1)
    spread(f2, gmt, hop1, sf2, 1, send=False)
    s2[2]()
    total = total_of(rb, n_grp) * scale
    sums[1] = total
    fin[mine, :] = total
    s3[1]()
    spread(f2, gmt, hop1, sf2, 1, compute=False)
    mixed(2, False)
    mixed(3, False)

    @pl.when(tm < n_tm - 1)
    def _():
        back_copy().wait_recv()

    grad_in(3, bpb[...])
    for ex in (q1[0], q1[1], q2[0], q2[1], f1[0], f1[1], s1, s2):
        ex[3]()

    @pl.when(tm < n_tm - 1)
    def _():
        next_copy().wait_send()

    @pl.when(tm > 0)
    def _():
        back_copy().wait_send()

    for h in range(2):
        f2[h][2]()
        hop(hop2, hop1, rf2, h)
        mixed(2 * h, True)
        mixed(2 * h + 1, True)
    s3[2]()
    for ex in (f2[0], f2[1], s3):
        ex[3]()


def finish(out_in, gin_in, fin, out_ref, gin_ref, gcw_ref, gcb_ref, gmw_ref, gmb_ref):
    out_ref[...] = out_in[...]
    gin_ref[...] = gin_in[...]
    two = fin[0:64, :].T
    gmw_ref[0] = two[0:64]
    gmw_ref[1] = two[64:128]
    gmw_ref[2] = fin[64:128, :].T[0:64]
    for tap in range(2):
        gcw_ref[tap] = fin[128 + 64 * tap : 192 + 64 * tap, :].T
    tail = fin[64:72, :]
    low = lax.broadcasted_iota(jnp.int32, (1, 128), 1) < 64
    gcb_ref[...] = jnp.where(low, pltpu.roll(tail[0:1], 64, 1), tail[1:2])
    gmb_ref[...] = pltpu.roll(tail[2:3], 64, 1)[:, 0:64]


def body(dims, inputs, grad_out, conv_w, conv_b, mix_w, mix_b, adj_tiles, tile_cols, send_rows, counts):
    x = inputs.reshape(512, 256)
    g = grad_out.reshape(512, 256)
    slot = lax.broadcasted_iota(jnp.int32, send_rows.shape[1:], 1)
    idx = jnp.where(slot < counts[0][:, None], send_rows[0], -1).reshape(1, -1)
    vmem = pl.BlockSpec(memory_space=pltpu.VMEM)
    smem = pl.BlockSpec(memory_space=pltpu.SMEM)
    hbm = pl.BlockSpec(memory_space=pltpu.HBM)
    n_space = dims[0]
    n_grp = dims[1] * dims[2]

    def bf(*shape):
        return pltpu.VMEM(shape, BF16)

    def fl(*shape):
        return pltpu.VMEM(shape, F32)

    def dma(*shape):
        return pltpu.SemaphoreType.DMA(shape)

    scratch = [
        bf(512, 256), bf(512, 256), bf(2, 8, 128, 128), bf(128, 256), bf(256, 256), bf(256, 640), bf(256, 512),
        bf(256, 256), bf(256, 256), bf(128, 384), bf(384, 128),
        bf(256, 1024), bf(1024, 256), bf(256, 1280), bf(1024, 256), bf(256, 256), bf(256, 512),
        bf(256, 512), bf(256, 512), fl(256, 512), fl(256, 512), bf(256, 512), bf(512, 256),
        bf(256, 512), bf(256, 512), bf(256, 1024), fl(512, 256),
    ]
    scratch += [bf(2, 1024, 256)] * 8
    scratch += [fl(256, 128)] * 3 + [fl(2, CHUNK, 128)]
    scratch += [dma(8, n_space), dma(8, n_space), dma(3, n_grp), dma(3, n_grp), dma(4), dma(3)]
    out, gin, fin = pl.pallas_call(
        functools.partial(kernel, dims),
        out_shape=(
            jax.ShapeDtypeStruct((512, 256), BF16),
            jax.ShapeDtypeStruct((512, 256), BF16),
            jax.ShapeDtypeStruct((256, 128), F32),
        ),
        in_specs=[hbm] * 3 + [vmem] * 4 + [smem, vmem],
        out_specs=(vmem,) * 3,
        scratch_shapes=scratch,
        compiler_params=pltpu.CompilerParams(
            collective_id=0, has_side_effects=True, vmem_limit_bytes=48 * 2**20
        ),
    )(x, g, adj_tiles, conv_w, conv_b.reshape(1, 128), mix_w, mix_b.reshape(1, 64), tile_cols, idx)
    out, gin, gcw, gcb, gmw, gmb = pl.pallas_call(
        finish,
        out_shape=(
            jax.ShapeDtypeStruct((512, 256), BF16),
            jax.ShapeDtypeStruct((512, 256), BF16),
            jax.ShapeDtypeStruct((2, 128, 64), F32),
            jax.ShapeDtypeStruct((1, 128), F32),
            jax.ShapeDtypeStruct((3, 64, 64), F32),
            jax.ShapeDtypeStruct((1, 64), F32),
        ),
        in_specs=[vmem] * 3,
        out_specs=(vmem,) * 6,
    )(out, gin, fin)
    return (
        out.reshape(inputs.shape),
        gin.reshape(inputs.shape),
        gcw,
        gcb.reshape(128),
        gmw,
        gmb.reshape(64),
    )


def solution(mesh):
    in_specs = (
        P("dp", "tm", None, "space"),
        P("dp", "tm", None, "space"),
        P(),
        P(),
        P(),
        P(),
        P("space", None, None, None),
        P("space", None),
        P("space", None, None),
        P("space", None),
    )
    out_specs = (P("dp", "tm", None, "space"), P("dp", "tm", None, "space"), P(), P(), P(), P())
    cells = 8 * 256 * mesh.shape["dp"] * mesh.shape["space"] * mesh.shape["tm"]
    dims = (mesh.shape["space"], mesh.shape["dp"], mesh.shape["tm"], 1.0 / math.sqrt(cells))
    return jax.shard_map(
        functools.partial(body, dims), mesh=mesh, in_specs=in_specs, out_specs=out_specs, check_vma=False
    )
```

time: 141 us -> 131 us (0.929); the launches traced: 141 us -> 129 us
  Pallas kernels: 132 us -> 120 us
    pallas_call x1, Pallas kernels: 132 us -> 118 us  [body(): pl.pallas_call(functools.partial(kernel, dims), out_shape=(jax.ShapeDtype...]
    pallas_call x0 -> x1, Pallas kernels: none -> 2.01 us  [body(): pl.pallas_call(finish, out_shape=(jax.ShapeDtypeStruct((512, 256), BF16),...]
    unnamed x25 -> x26, local copies, waits for them, and re-layouts: 7.5 us -> 7.36 us
where the time goes in v2:
time: 131 us; the launch traced here: 129 us
  Pallas kernels  120 us (92%)
  local copies, waits for them, and re-layouts  7.53 us (6%)
    pallas_call x1, Pallas kernels, body(): pl.pallas_call(functools.partial(kernel, dims), out_shape=(jax.ShapeDtype...  118 us
    unnamed x26, local copies, waits for them, and re-layouts  7.36 us

profile of v2, /device:TPU:1, one launch (start us, length us, event | category | flops | bytes accessed | tf_op | source)
XLA Modules:
  0.0 129.0 jit_solution(10825685504354588703)
XLA Ops:
  0.6 0.0 copy-start.11
  0.6 0.0 copy-start.10
  0.7 0.7 iota_compare_fusion
  1.4 0.1 lt.23
  1.5 0.0 copy-done.11
  1.5 0.1 squeeze.3
  1.6 0.0 copy-done.10
  1.6 0.0 copy-start.6
  1.6 0.0 copy-start.7
  1.6 0.0 copy-start.8
  1.6 0.0 copy-start.9
  1.6 0.1 copy.16.convw_ref
  1.8 0.6 copy-done.6
  2.4 0.0 copy-done.7
  2.4 0.0 copy-done.8
  2.4 0.0 copy-done.9
  2.4 0.0 copy-start
  2.4 1.0 copy-done
  3.4 0.0 copy-start.3
  3.4 0.9 copy-done.3
  4.4 0.0 copy-start.4
  4.4 0.9 copy-done.4
  5.3 117.9 %shard_map.145 = (bf16[512,256]{1,0:T(8,128)(2,1)S(1)}, bf16[512,256]{1,0:T(8,128)(2,1)S(1)}, f32[256,128]{1,0:T(8,128)S(1)}) custom-call(bf16[512,256]{1,0:T(8,128)(2,1)S(1)} %bitcast.9, bf16[512,256]{1,0:T(8,128)(2,1)S(1)} %bitcast.10, bf16[2,8,128,128]{3,2,1,0:T(8,128)(2,1)S(1)} %copy-done, bf16[2,128,64]{2,1,0:T(8,128)(2,1)S(1)} %copy.16.convw_ref, ...), custom_call_target="tpu_custom_call" | custom-call | tf_op jit(solution)/shard_map/pallas_call | solution.py:460
  123.3 0.0 copy-start.1
  123.3 0.7 copy-done.1
  124.0 0.0 copy-start.2
  124.0 0.7 copy-done.2
  124.7 0.0 copy-start.5
  124.7 0.6 copy-done.5
  125.3 2.0 %shard_map.146 = (bf16[512,256]{1,0:T(8,128)(2,1)}, bf16[512,256]{1,0:T(8,128)(2,1)}, f32[2,128,64]{2,1,0:T(8,128)}, f32[1,128]{1,0:T(1,128)}, f32[3,64,64]{2,1,0:T(8,128)}, /*index=5*/f32[1,64]{1,0:T(1,128)}) custom-call(bf16[512,256]{1,0:T(8,128)(2,1)} %copy-done.1, bf16[512,256]{1,0:T(8,128)(2,1)} %copy-done.2, f32[256,128]{1,0:T(8,128)} %copy-done.5), custom_call_target="tpu_custom_call" | custom-call | tf_op jit(solution)/shard_map/pallas_call | solution.py:474
  127.3 1.6 %copy.17 = f32[2,128,64]{1,2,0:T(8,128)} copy(f32[2,128,64]{2,1,0:T(8,128)} %get-tuple-element.26) | data formatting | bytes 131072
  (1 shorter events, 0.0 us)
Async XLA Ops:
  0.6 0.9 copy-start.11
  0.6 0.9 copy-start.10
  1.6 0.8 copy-start.6
  1.6 0.8 copy-start.7
  1.6 0.8 copy-start.8
  1.6 0.8 copy-start.9
  2.4 1.0 copy-start
  3.4 0.9 copy-start.3
  4.4 0.9 copy-start.4
  123.3 0.7 copy-start.1
  124.0 0.7 copy-start.2
  124.7 0.6 copy-start.5

commit v3 on v2

--- a/solution.py
+++ b/solution.py
@@ -12,7 +12,6 @@
 F32 = jnp.float32
 BF16 = jnp.bfloat16
 SLOTS = 64
-CHUNK = 16
 
 
 def nn(a, b):
@@ -54,32 +53,49 @@
 
 def kernel(
     dims,
-    x_hbm, g_hbm, adj_hbm, convw_ref, convb_ref, mixw_ref, mixb_ref, cols_ref, idx_ref,
+    x_hbm, g_hbm, adj_hbm, convw_hbm, convb_hbm, mixw_hbm, mixb_hbm, send_hbm, cols_ref, counts_ref,
     out_ref, gin_ref, fin,
-    x_ref, g_ref, adj_ref, xb, bpb, xt, gt, wt, wtt, mcat, mcatv, gm, gmt, dm, dmt, dlo, dlot,
+    x_ref, g_ref, adj_ref, convw_ref, convb_ref, mixw_ref, mixb_ref, send_ref, xb, bpb, xt, gt, wt, wtt, mcat, mcatv, gm, gmt, dm, dmt, dlo, dlot,
     qg, qqg, filt, gate, hid, hidn, hop1, hop2, bp, part,
     sq1, sq2, sf1, sf2, rq1, rq2, rf1, rf2,
-    pay, ra, rb, sums,
+    pay, ra, rb, rc, rd, sum_a, sum_b, sum_c,
     ssem, rsem, assem, arsem, nsem, lsem,
 ):
     n_space, n_dp, n_tm, scale = dims
     me = lax.axis_index("space")
     tm = lax.axis_index("tm")
     dp = lax.axis_index("dp")
-    grp = dp * n_tm + tm
-    n_grp = n_dp * n_tm
     z = lax.div(me, 4)
     y = lax.rem(me, 4)
+    z_hi = lax.div(tm, 2)
+    core = lax.rem(tm, 2)
+    e = dp * 2 + core
+    n_e = n_dp * 2
+    q = z_hi * 4 + z
 
     def space_dev(k):
         return {"space": k}
 
-    def grp_dev(k):
-        return {"dp": lax.div(k, n_tm), "tm": lax.rem(k, n_tm)}
+    def e_dev(k):
+        return {"dp": lax.div(k, 2), "tm": z_hi * 2 + lax.rem(k, 2)}
+
+    def y_dev(k):
+        return {"space": z * 4 + k}
+
+    def q_dev(k):
+        return {"space": lax.rem(k, 4) * 4 + y, "tm": lax.div(k, 4) * 2 + core}
+
+    def signal(dev):
+        pl.semaphore_signal(barrier, inc=1, device_id=dev, device_id_type=MESH)
 
     loads = [
         pltpu.make_async_copy(src, dst, lsem.at[i])
-        for i, (src, dst) in enumerate(((g_hbm, g_ref), (adj_hbm, adj_ref), (x_hbm, x_ref)))
+        for i, (src, dst) in enumerate(
+            (
+                (g_hbm, g_ref), (adj_hbm, adj_ref), (x_hbm, x_ref), (send_hbm, send_ref),
+                (convw_hbm, convw_ref), (convb_hbm, convb_ref), (mixw_hbm, mixw_ref), (mixb_hbm, mixb_ref),
+            )
+        )
     ]
     for load in loads:
         load.start()
@@ -88,15 +104,17 @@
 
     @pl.loop(1, n_space)
     def _(off):
-        pl.semaphore_signal(
-            barrier, inc=1, device_id=space_dev(lax.rem(me + off, n_space)), device_id_type=MESH
-        )
-
-    @pl.loop(1, n_grp)
+        signal(space_dev(lax.rem(me + off, n_space)))
+
+    @pl.loop(1, n_e)
     def _(off):
-        pl.semaphore_signal(
-            barrier, inc=1, device_id=grp_dev(lax.rem(grp + off, n_grp)), device_id_type=MESH
-        )
+        signal(e_dev(lax.rem(e + off, n_e)))
+
+    @pl.loop(0, 4)
+    def _(k):
+        signal(q_dev((1 - z_hi) * 4 + k))
+
+    signal({"tm": 3 - tm})
 
     def halo(i, send, recv):
         return [
@@ -171,8 +189,9 @@
     for ref in (rq1, rq2, rf1, rf2):
         for h in range(2):
             ref[h, own_slots, :] = jnp.zeros((SLOTS, 256), BF16)
-    loads[2].wait()
-    pl.semaphore_wait(barrier, n_space - 1 + n_grp - 1)
+    for load in loads[2:]:
+        load.wait()
+    pl.semaphore_wait(barrier, n_space - 1 + n_e - 1 + 4 + 1)
 
     for h in range(2):
         spread(q1, dmt, gt, sq1, h)
@@ -200,12 +219,15 @@
             dlot[128 * b : 128 * (b + 1), 128 * r : 128 * (r + 1)] = high.T
             dlot[128 * b : 128 * (b + 1), 256 + 128 * r : 256 + 128 * (r + 1)] = low.T
 
-    for m in range(4):
-        lanes = slice(256 * m, 256 * (m + 1))
-        sensor = lax.broadcasted_iota(jnp.int32, (256, 256), 0)
-        block = (sensor == idx_ref[0:1, lanes]).astype(F32).astype(BF16)
-        gm[:, lanes] = block
-        gmt[lanes, :] = block.T
+    slot = lax.broadcasted_iota(jnp.int32, (1, SLOTS), 1)
+    sensor = lax.broadcasted_iota(jnp.int32, (256, 128), 0)
+    for m in range(8):
+        picks = [
+            jnp.where(slot < counts_ref[0, d], send_ref[d : d + 1, :], -1) for d in (2 * m, 2 * m + 1)
+        ]
+        block = (sensor == jnp.concatenate(picks, 1)).astype(F32).astype(BF16)
+        gm[:, 128 * m : 128 * (m + 1)] = block
+        gmt[128 * m : 128 * (m + 1), :] = block.T
 
     zero = jnp.zeros((64, 64), F32)
 
@@ -219,9 +241,9 @@
         mcatv[128 * k : 128 * (k + 1), :] = block
     for half in range(2):
         for tap in range(2):
-            block = pair(convw_ref[tap, 64 * half : 64 * (half + 1), :]).astype(BF16)
-            wt[128 * half : 128 * (half + 1), 128 * tap : 128 * (tap + 1)] = block
-            wtt[128 * tap : 128 * (tap + 1), 128 * half : 128 * (half + 1)] = block.T
+            block = pair(convw_ref[tap].astype(F32)[:, 64 * half : 64 * (half + 1)]).astype(BF16)
+            wtt[128 * tap : 128 * (tap + 1), 128 * half : 128 * (half + 1)] = block
+            wt[128 * half : 128 * (half + 1), 128 * tap : 128 * (tap + 1)] = block.T
 
     for p in range(4):
         xt[:, 128 * (p + 1) : 128 * (p + 2)] = x_ref[128 * p : 128 * (p + 1), :].T
@@ -251,7 +273,7 @@
         spread(q2, dmt, qg, sq2, h)
 
     spread(f1, gmt, hid, sf1, 0)
-    spread(f1, gmt, hid, sf1, 1, send=False)
+    spread(f1, gmt, hid, sf1, 1)
     for p in range(4):
         lanes = slice(128 * p, 128 * (p + 1))
         hidn[lanes, :] = hid[:, lanes].T
@@ -320,21 +342,23 @@
             low_lanes, diag_low(acc[:, :128]), diag_high(acc[:, 128:])
         )
 
-    s1 = exchange(me, n_space, space_dev, rows(pay, CHUNK), rows(ra, CHUNK), assem.at[0], arsem.at[0])
-    s2 = exchange(grp, n_grp, grp_dev, lambda k: sums.at[0], rows(rb, CHUNK), assem.at[1], arsem.at[1])
-    s3 = exchange(me, n_space, space_dev, lambda k: sums.at[1], rows(fin, CHUNK), assem.at[2], arsem.at[2])
-    mine = pl.ds(pl.multiple_of(me * CHUNK, CHUNK), CHUNK)
-    ours = pl.ds(pl.multiple_of(grp * CHUNK, CHUNK), CHUNK)
-
-    def total_of(ref, count):
-        total = ref[0:CHUNK, :]
+    s1 = exchange(e, n_e, e_dev, rows(pay, 32), rows(ra, 32), assem.at[0], arsem.at[0])
+    s2 = exchange(y, 4, y_dev, rows(sum_a, 8), rows(rb, 8), assem.at[1], arsem.at[1])
+    s3 = exchange(q, 8, q_dev, lambda k: sum_b, rows(rc, 8), assem.at[2], arsem.at[2])
+    s4 = exchange(y, 4, y_dev, lambda k: sum_c, rows(rd, 8), assem.at[3], arsem.at[3])
+    s5 = exchange(e, n_e, e_dev, lambda k: rd, rows(fin, 32), assem.at[4], arsem.at[4])
+
+    def total_of(ref, count, size):
+        total = ref[0:size, :]
         for k in range(1, count):
-            total = total + ref[CHUNK * k : CHUNK * (k + 1), :]
+            total = total + ref[size * k : size * (k + 1), :]
         return total
 
-    ra[mine, :] = pay[mine, :]
+    def place(k, size):
+        return pl.ds(pl.multiple_of(k * size, size), size)
+
+    ra[place(e, 32), :] = pay[place(e, 32), :]
     s1[1]()
-    spread(f1, gmt, hid, sf1, 1, compute=False)
 
     def grad_in(p, nxt):
         lanes = slice(128 * p, 128 * (p + 1))
@@ -349,10 +373,14 @@
         grad_in(p, bp[:, 256 * (p + 1) : 256 * (p + 2)])
 
     s1[2]()
-    total = total_of(ra, n_space)
-    sums[0] = total
-    rb[ours, :] = total
+    sum_a[...] = total_of(ra, n_e, 32)
+    rb[place(y, 8), :] = sum_a[place(y, 8), :]
     s2[1]()
+    s2[2]()
+    total = total_of(rb, 4, 8)
+    sum_b[...] = total
+    rc[place(q, 8), :] = total
+    s3[1]()
 
     def hop(dst, src, recv, h):
         lanes = slice(256 * h, 256 * (h + 1))
@@ -376,22 +404,24 @@
     mixed(1, False)
     f1[1][2]()
     hop(hop1, hid, rf1, 1)
-    spread(f2, gmt, hop1, sf2, 1, send=False)
-    s2[2]()
-    total = total_of(rb, n_grp) * scale
-    sums[1] = total
-    fin[mine, :] = total
-    s3[1]()
-    spread(f2, gmt, hop1, sf2, 1, compute=False)
+    spread(f2, gmt, hop1, sf2, 1)
+    s3[2]()
+    total = total_of(rc, 8, 8) * scale
+    sum_c[...] = total
+    rd[place(y, 8), :] = total
+    s4[1]()
     mixed(2, False)
     mixed(3, False)
+    s4[2]()
+    fin[place(e, 32), :] = rd[...]
+    s5[1]()
 
     @pl.when(tm < n_tm - 1)
     def _():
         back_copy().wait_recv()
 
     grad_in(3, bpb[...])
-    for ex in (q1[0], q1[1], q2[0], q2[1], f1[0], f1[1], s1, s2):
+    for ex in (q1[0], q1[1], q2[0], q2[1], f1[0], f1[1], s1, s2, s3, s4):
         ex[3]()
 
     @pl.when(tm < n_tm - 1)
@@ -407,8 +437,8 @@
         hop(hop2, hop1, rf2, h)
         mixed(2 * h, True)
         mixed(2 * h + 1, True)
-    s3[2]()
-    for ex in (f2[0], f2[1], s3):
+    s5[2]()
+    for ex in (f2[0], f2[1], s5):
         ex[3]()
 
 
@@ -420,7 +450,7 @@
     gmw_ref[1] = two[64:128]
     gmw_ref[2] = fin[64:128, :].T[0:64]
     for tap in range(2):
-        gcw_ref[tap] = fin[128 + 64 * tap : 192 + 64 * tap, :].T
+        gcw_ref[tap] = fin[128 + 64 * tap : 192 + 64 * tap, :]
     tail = fin[64:72, :]
     low = lax.broadcasted_iota(jnp.int32, (1, 128), 1) < 64
     gcb_ref[...] = jnp.where(low, pltpu.roll(tail[0:1], 64, 1), tail[1:2])
@@ -430,13 +460,11 @@
 def body(dims, inputs, grad_out, conv_w, conv_b, mix_w, mix_b, adj_tiles, tile_cols, send_rows, counts):
     x = inputs.reshape(512, 256)
     g = grad_out.reshape(512, 256)
-    slot = lax.broadcasted_iota(jnp.int32, send_rows.shape[1:], 1)
-    idx = jnp.where(slot < counts[0][:, None], send_rows[0], -1).reshape(1, -1)
     vmem = pl.BlockSpec(memory_space=pltpu.VMEM)
     smem = pl.BlockSpec(memory_space=pltpu.SMEM)
     hbm = pl.BlockSpec(memory_space=pltpu.HBM)
     n_space = dims[0]
-    n_grp = dims[1] * dims[2]
+    n_e = dims[1] * 2
 
     def bf(*shape):
         return pltpu.VMEM(shape, BF16)
@@ -448,15 +476,16 @@
         return pltpu.SemaphoreType.DMA(shape)
 
     scratch = [
-        bf(512, 256), bf(512, 256), bf(2, 8, 128, 128), bf(128, 256), bf(256, 256), bf(256, 640), bf(256, 512),
+        bf(512, 256), bf(512, 256), bf(2, 8, 128, 128), bf(2, 64, 128), fl(1, 128), bf(3, 64, 64), fl(1, 64),
+        pltpu.VMEM((16, SLOTS), jnp.int32), bf(128, 256), bf(256, 256), bf(256, 640), bf(256, 512),
         bf(256, 256), bf(256, 256), bf(128, 384), bf(384, 128),
         bf(256, 1024), bf(1024, 256), bf(256, 1280), bf(1024, 256), bf(256, 256), bf(256, 512),
         bf(256, 512), bf(256, 512), fl(256, 512), fl(256, 512), bf(256, 512), bf(512, 256),
         bf(256, 512), bf(256, 512), bf(256, 1024), fl(512, 256),
     ]
     scratch += [bf(2, 1024, 256)] * 8
-    scratch += [fl(256, 128)] * 3 + [fl(2, CHUNK, 128)]
-    scratch += [dma(8, n_space), dma(8, n_space), dma(3, n_grp), dma(3, n_grp), dma(4), dma(3)]
+    scratch += [fl(256, 128), fl(256, 128), fl(32, 128), fl(64, 128), fl(32, 128), fl(32, 128), fl(8, 128), fl(8, 128)]
+    scratch += [dma(8, n_space), dma(8, n_space), dma(5, n_e), dma(5, n_e), dma(4), dma(8)]
     out, gin, fin = pl.pallas_call(
         functools.partial(kernel, dims),
         out_shape=(
@@ -464,19 +493,22 @@
             jax.ShapeDtypeStruct((512, 256), BF16),
             jax.ShapeDtypeStruct((256, 128), F32),
         ),
-        in_specs=[hbm] * 3 + [vmem] * 4 + [smem, vmem],
+        in_specs=[hbm] * 8 + [smem] * 2,
         out_specs=(vmem,) * 3,
         scratch_shapes=scratch,
         compiler_params=pltpu.CompilerParams(
-            collective_id=0, has_side_effects=True, vmem_limit_bytes=48 * 2**20
+            collective_id=0, has_side_effects=True, vmem_limit_bytes=60 * 2**20
         ),
-    )(x, g, adj_tiles, conv_w, conv_b.reshape(1, 128), mix_w, mix_b.reshape(1, 64), tile_cols, idx)
+    )(
+        x, g, adj_tiles, jnp.swapaxes(conv_w, 1, 2), conv_b.reshape(1, 128), mix_w, mix_b.reshape(1, 64),
+        send_rows[0], tile_cols, counts,
+    )
     out, gin, gcw, gcb, gmw, gmb = pl.pallas_call(
         finish,
         out_shape=(
             jax.ShapeDtypeStruct((512, 256), BF16),
             jax.ShapeDtypeStruct((512, 256), BF16),
-            jax.ShapeDtypeStruct((2, 128, 64), F32),
+            jax.ShapeDtypeStruct((2, 64, 128), F32),
             jax.ShapeDtypeStruct((1, 128), F32),
             jax.ShapeDtypeStruct((3, 64, 64), F32),
             jax.ShapeDtypeStruct((1, 64), F32),
@@ -487,7 +519,7 @@
     return (
         out.reshape(inputs.shape),
         gin.reshape(inputs.shape),
-        gcw,
+        jnp.swapaxes(gcw, 1, 2),
         gcb.reshape(128),
         gmw,
         gmb.reshape(64),

time: 131 us -> 113 us (0.86)
  Pallas kernels: 120 us -> 111 us
  local copies, waits for them, and re-layouts: 7.53 us -> 0 us
    pallas_call x1, Pallas kernels: 118 us -> 109 us  [body(): pl.pallas_call(functools.partial(kernel, dims), out_shape=(jax.ShapeDtype...]
    unnamed x26 -> x0, local copies, waits for them, and re-layouts: 7.36 us -> none
where the time goes in v3:
time: 113 us; the launch traced here: 111 us
  Pallas kernels  111 us (98%)
    pallas_call x1, Pallas kernels, body(): pl.pallas_call(functools.partial(kernel, dims), out_shape=(jax.ShapeDtype...  109 us

profile of v3, /device:TPU:1, one launch (start us, length us, event | category | flops | bytes accessed | tf_op | source)
XLA Modules:
  0.0 111.3 jit_solution(9186158580783011336)
XLA Ops:
  0.6 108.7 %shard_map.145 = (bf16[512,256]{1,0:T(8,128)(2,1)}, bf16[512,256]{1,0:T(8,128)(2,1)}, f32[256,128]{1,0:T(8,128)}) custom-call(bf16[512,256]{1,0:T(8,128)(2,1)} %bitcast.11, bf16[512,256]{1,0:T(8,128)(2,1)} %bitcast.12, bf16[2,8,128,128]{3,2,1,0:T(8,128)(2,1)} %adj_hbm.1, bf16[2,64,128]{2,1,0:T(8,128)(2,1)} %bitcast.13, f32[1,128]{1,0:T(1,128)} %bitcast.15, ...), custom_call_target="tpu_custom_call" | custom-call | tf_op jit(solution)/shard_map/pallas_call | solution.py:489
  109.4 1.9 %shard_map.146 = (bf16[512,256]{1,0:T(8,128)(2,1)}, bf16[512,256]{1,0:T(8,128)(2,1)}, f32[2,64,128]{2,1,0:T(8,128)}, f32[1,128]{1,0:T(1,128)}, f32[3,64,64]{2,1,0:T(8,128)}, /*index=5*/f32[1,64]{1,0:T(1,128)}) custom-call(bf16[512,256]{1,0:T(8,128)(2,1)} %get-tuple-element.15.out_in, bf16[512,256]{1,0:T(8,128)(2,1)} %get-tuple-element.16.gin_in, ...), custom_call_target="tpu_custom_call" | custom-call | tf_op jit(solution)/shard_map/pallas_call | solution.py:506

commit v4 on v3

--- a/solution.py
+++ b/solution.py
@@ -59,7 +59,8 @@
     qg, qqg, filt, gate, hid, hidn, hop1, hop2, bp, part,
     sq1, sq2, sf1, sf2, rq1, rq2, rf1, rf2,
     pay, ra, rb, rc, rd, sum_a, sum_b, sum_c,
-    ssem, rsem, assem, arsem, nsem, lsem,
+    meta, metax, gx, gxt, far, pick, rx1, rx2, tsend, tback,
+    ssem, rsem, assem, arsem, nsem, lsem, fsem, psem, xsem,
 ):
     n_space, n_dp, n_tm, scale = dims
     me = lax.axis_index("space")
@@ -72,6 +73,12 @@
     e = dp * 2 + core
     n_e = n_dp * 2
     q = z_hi * 4 + z
+    side = lax.div(z, 2)
+    end_z = 3 * side
+    far_z = 3 - end_z
+    is_end = z == end_z
+    far_me = far_z * 4 + y
+    row_in_side = lax.rem(z, 2) * 4 + y
 
     def space_dev(k):
         return {"space": k}
@@ -135,17 +142,25 @@
         odd = lax.rem(lax.div(step + 1, 2), 2)
         return 2 * lax.rem(lax.div(z, 2) + far, 2) + lax.rem(lax.rem(z, 2) + odd, 2)
 
-    def spread(ex, matrix, field, buf, h, compute=True, send=True):
+    def slot_block(ref, h, k):
+        return ref.at[h, pl.ds(pl.multiple_of(k * SLOTS, SLOTS), SLOTS), :]
+
+    def across(part):
+        return is_end & (lax.div(part, 8) != side)
+
+    def f_spread(ex, field, buf, h):
         copy = ex[h][0]
         lanes = slice(256 * h, 256 * (h + 1))
 
         @pl.loop(0, 4)
         def _(step):
             zz = by_distance(step)
-            if compute:
+
+            @pl.when(jnp.logical_not(across(zz * 4)))
+            def _():
                 at = pl.ds(pl.multiple_of(zz * 256, 256), 256)
-                buf[h, at, :] = nn(matrix[at, :], field[:, lanes]).astype(BF16)
-            if send:
+                buf[h, at, :] = nn(gmt[at, :], field[:, lanes]).astype(BF16)
+
                 @pl.loop(0, 4)
                 def _(k):
                     tgt = zz * 4 + lax.rem(y + k, 4)
@@ -153,6 +168,171 @@
                     @pl.when(tgt != me)
                     def _():
                         copy(tgt, me).start()
+
+    def swap(i, h, field):
+        return pltpu.make_async_remote_copy(
+            src_ref=field.at[:, pl.ds(256 * h, 256)], dst_ref=far.at[2 * i + h],
+            send_sem=fsem.at[0, 2 * i + h], recv_sem=fsem.at[1, 2 * i + h],
+            device_id=space_dev(far_me), device_id_type=MESH,
+        )
+
+    def f_swap(i, h, field):
+        @pl.when(is_end)
+        def _():
+            swap(i, h, field).start()
+
+    def proxy_copy(i, h, recv, k, tgt):
+        return pltpu.make_async_remote_copy(
+            src_ref=slot_block(pick, 2 * i + h, k), dst_ref=slot_block(recv, h, far_me),
+            send_sem=psem.at[2 * i + h, k], recv_sem=rsem.at[4 + 2 * i + h, far_me],
+            device_id=space_dev(tgt), device_id_type=MESH,
+        )
+
+    def f_proxy(i, h, field, recv):
+        @pl.when(is_end)
+        def _():
+            swap(i, h, field).wait_recv()
+
+            @pl.loop(0, 2)
+            def _(step):
+                zz = lax.rem(lax.rem(z, 2) + 1 + step, 2)
+                at = pl.ds(pl.multiple_of(zz * 256, 256), 256)
+                pick[2 * i + h, at, :] = nn(gxt[at, :], far[2 * i + h]).astype(BF16)
+
+                @pl.loop(0, 4)
+                def _(j):
+                    k = zz * 4 + lax.rem(y + j, 4)
+                    tgt = side * 8 + k
+
+                    @pl.when(tgt != me)
+                    def _():
+                        proxy_copy(i, h, recv, k, tgt).start()
+
+            slot_block(recv, h, far_me)[...] = slot_block(pick, 2 * i + h, row_in_side)[...]
+
+    def f_received(i, h, ex):
+        copy = ex[h][0]
+
+        @pl.loop(1, n_space)
+        def _(off):
+            frm = lax.rem(me + (n_space - off), n_space)
+
+            @pl.when(jnp.logical_not(is_end & (frm == far_me)))
+            def _():
+                copy(lax.rem(me + off, n_space), frm).wait_recv()
+
+    def f_sent(i, h, ex, field, recv):
+        copy = ex[h][0]
+
+        @pl.loop(1, n_space)
+        def _(off):
+            tgt = lax.rem(me + off, n_space)
+
+            @pl.when(jnp.logical_not(across(tgt)))
+            def _():
+                copy(tgt, me).wait_send()
+
+        @pl.when(is_end)
+        def _():
+            swap(i, h, field).wait_send()
+
+            @pl.loop(0, 8)
+            def _(k):
+                @pl.when(k != row_in_side)
+                def _():
+                    proxy_copy(i, h, recv, k, side * 8 + k).wait_send()
+
+    def collect_copy(i, h, send, rx, s, k):
+        return pltpu.make_async_remote_copy(
+            src_ref=slot_block(send, h, s), dst_ref=slot_block(rx, h, k),
+            send_sem=ssem.at[2 * i + h, s], recv_sem=xsem.at[2 * i + h, k],
+            device_id=space_dev(end_z * 4 + lax.rem(s, 4)), device_id_type=MESH,
+        )
+
+    def q_spread(i, ex, field, buf, rx, h):
+        copy = ex[h][0]
+        lanes = slice(256 * h, 256 * (h + 1))
+
+        @pl.loop(0, 4)
+        def _(step):
+            zz = by_distance(step)
+            at = pl.ds(pl.multiple_of(zz * 256, 256), 256)
+            buf[h, at, :] = nn(dmt[at, :], field[:, lanes]).astype(BF16)
+
+            @pl.loop(0, 4)
+            def _(k):
+                tgt = zz * 4 + lax.rem(y + k, 4)
+
+                @pl.when((zz != far_z) & (tgt != me))
+                def _():
+                    copy(tgt, me).start()
+
+                @pl.when((zz == far_z) & (jnp.logical_not(is_end) | (tgt != far_me)))
+                def _():
+                    collect_copy(i, h, buf, rx, tgt, row_in_side).start()
+
+        @pl.when(is_end)
+        def _():
+            slot_block(rx, h, row_in_side)[...] = slot_block(buf, h, far_me)[...]
+
+    def back_field(i, h):
+        return pltpu.make_async_remote_copy(
+            src_ref=tsend.at[2 * i + h], dst_ref=tback.at[2 * i + h],
+            send_sem=fsem.at[2, 2 * i + h], recv_sem=fsem.at[3, 2 * i + h],
+            device_id=space_dev(far_me), device_id_type=MESH,
+        )
+
+    def q_received(i, h, ex, buf, rx):
+        copy = ex[h][0]
+
+        @pl.when(is_end)
+        def _():
+            @pl.loop(0, 8)
+            def _(k):
+                @pl.when(k != row_in_side)
+                def _():
+                    collect_copy(i, h, buf, rx, far_me, k).wait_recv()
+
+            tsend[2 * i + h] = nn(gx[...], rx[h]).astype(BF16)
+            back_field(i, h).start()
+
+        @pl.loop(1, n_space)
+        def _(off):
+            frm = lax.rem(me + (n_space - off), n_space)
+
+            @pl.when(jnp.logical_not(across(frm)))
+            def _():
+                copy(lax.rem(me + off, n_space), frm).wait_recv()
+
+        @pl.when(is_end)
+        def _():
+            back_field(i, h).wait_recv()
+
+    def q_sent(i, h, ex, buf, rx):
+        copy = ex[h][0]
+
+        @pl.loop(1, n_space)
+        def _(off):
+            tgt = lax.rem(me + off, n_space)
+            zz = lax.div(tgt, 4)
+
+            @pl.when(zz != far_z)
+            def _():
+                copy(tgt, me).wait_send()
+
+            @pl.when((zz == far_z) & (jnp.logical_not(is_end) | (tgt != far_me)))
+            def _():
+                collect_copy(i, h, buf, rx, tgt, row_in_side).wait_send()
+
+        @pl.when(is_end)
+        def _():
+            back_field(i, h).wait_send()
+
+    def meta_copy():
+        return pltpu.make_async_remote_copy(
+            src_ref=meta, dst_ref=metax, send_sem=nsem.at[4], recv_sem=nsem.at[5],
+            device_id=space_dev(far_me), device_id_type=MESH,
+        )
 
     def next_copy():
         return pltpu.make_async_remote_copy(
@@ -189,12 +369,30 @@
     for ref in (rq1, rq2, rf1, rf2):
         for h in range(2):
             ref[h, own_slots, :] = jnp.zeros((SLOTS, 256), BF16)
+    @pl.when(is_end)
+    def _():
+        for ref in (rq1, rq2):
+            for h in range(2):
+                ref[h, pl.ds(pl.multiple_of((1 - side) * 512, 512), 512), :] = jnp.zeros((512, 256), BF16)
+
+    @pl.when(jnp.logical_not(is_end))
+    def _():
+        tback[...] = jnp.zeros_like(tback)
+
     for load in loads[2:]:
         load.wait()
+    slot = lax.broadcasted_iota(jnp.int32, (1, SLOTS), 1)
+    for d in range(16):
+        picks = jnp.where(slot < counts_ref[0, d], send_ref[d : d + 1, :], -1)
+        meta[d : d + 1, :] = jnp.concatenate([picks, picks], 1)
     pl.semaphore_wait(barrier, n_space - 1 + n_e - 1 + 4 + 1)
 
-    for h in range(2):
-        spread(q1, dmt, gt, sq1, h)
+    @pl.when(is_end)
+    def _():
+        meta_copy().start()
+
+    for h in range(2):
+        q_spread(0, q1, gt, sq1, rx1, h)
 
     @pl.when(tm < n_tm - 1)
     def _():
@@ -219,15 +417,16 @@
             dlot[128 * b : 128 * (b + 1), 128 * r : 128 * (r + 1)] = high.T
             dlot[128 * b : 128 * (b + 1), 256 + 128 * r : 256 + 128 * (r + 1)] = low.T
 
-    slot = lax.broadcasted_iota(jnp.int32, (1, SLOTS), 1)
     sensor = lax.broadcasted_iota(jnp.int32, (256, 128), 0)
+    low_row = lax.broadcasted_iota(jnp.int32, (1, 128), 1) < 64
+
+    def select(first, second):
+        return (sensor == jnp.where(low_row, first, second)).astype(F32).astype(BF16)
+
     for m in range(8):
-        picks = [
-            jnp.where(slot < counts_ref[0, d], send_ref[d : d + 1, :], -1) for d in (2 * m, 2 * m + 1)
-        ]
-        block = (sensor == jnp.concatenate(picks, 1)).astype(F32).astype(BF16)
-        gm[:, 128 * m : 128 * (m + 1)] = block
-        gmt[128 * m : 128 * (m + 1), :] = block.T
+        sel = select(meta[2 * m : 2 * m + 1, :], meta[2 * m + 1 : 2 * m + 2, :])
+        gm[:, 128 * m : 128 * (m + 1)] = sel
+        gmt[128 * m : 128 * (m + 1), :] = sel.T
 
     zero = jnp.zeros((64, 64), F32)
 
@@ -265,15 +464,29 @@
         hid[:, lanes] = (f * s).astype(BF16)
 
     for h in range(2):
+        f_swap(0, h, hid)
+
+    @pl.when(is_end)
+    def _():
+        meta_copy().wait_recv()
+        for m in range(4):
+            d = side * 8 + 2 * m
+            sel = select(metax[pl.ds(d, 1), :], metax[pl.ds(d + 1, 1), :])
+            gx[:, 128 * m : 128 * (m + 1)] = sel
+            gxt[128 * m : 128 * (m + 1), :] = sel.T
+
+    for h in range(2):
         lanes = slice(256 * h, 256 * (h + 1))
-        q1[h][2]()
+        q_received(0, h, q1, sq1, rx1)
         grad = gt[:, lanes]
         own = nn(dlot[:, :256], grad) + nn(dlot[:, 256:], grad)
+        own = own + tback[h].astype(F32)
         qg[:, lanes] = (own + nn(gm[...], rq1[h])).astype(BF16)
-        spread(q2, dmt, qg, sq2, h)
-
-    spread(f1, gmt, hid, sf1, 0)
-    spread(f1, gmt, hid, sf1, 1)
+        q_spread(1, q2, qg, sq2, rx2, h)
+
+    for h in range(2):
+        f_spread(f1, hid, sf1, h)
+        f_proxy(0, h, hid, rf1)
     for p in range(4):
         lanes = slice(128 * p, 128 * (p + 1))
         hidn[lanes, :] = hid[:, lanes].T
@@ -297,9 +510,10 @@
 
     for h in range(2):
         lanes = slice(256 * h, 256 * (h + 1))
-        q2[h][2]()
+        q_received(1, h, q2, sq2, rx2)
         grad = qg[:, lanes]
         own = nn(dlot[:, :256], grad) + nn(dlot[:, 256:], grad)
+        own = own + tback[2 + h].astype(F32)
         qqg[:, lanes] = (own + nn(gm[...], rq2[h])).astype(BF16)
         for p in (2 * h, 2 * h + 1):
             lanes = slice(128 * p, 128 * (p + 1))
@@ -397,33 +611,40 @@
             here = nt(mcat[:, :128], hid[:, lanes]) + nt(mcat[:, 128:256], hop1[:, lanes])
             part[lanes, :] = x_ref[lanes, :].astype(F32) + mb + here
 
-    f1[0][2]()
-    hop(hop1, hid, rf1, 0)
-    spread(f2, gmt, hop1, sf2, 0)
-    mixed(0, False)
-    mixed(1, False)
-    f1[1][2]()
-    hop(hop1, hid, rf1, 1)
-    spread(f2, gmt, hop1, sf2, 1)
+    for h in range(2):
+        f_received(0, h, f1)
+        hop(hop1, hid, rf1, h)
+        f_swap(1, h, hop1)
+        f_spread(f2, hop1, sf2, h)
+    f_proxy(1, 0, hop1, rf2)
     s3[2]()
     total = total_of(rc, 8, 8) * scale
     sum_c[...] = total
     rd[place(y, 8), :] = total
     s4[1]()
-    mixed(2, False)
-    mixed(3, False)
+    f_proxy(1, 1, hop1, rf2)
     s4[2]()
     fin[place(e, 32), :] = rd[...]
     s5[1]()
+    for p in range(4):
+        mixed(p, False)
 
     @pl.when(tm < n_tm - 1)
     def _():
         back_copy().wait_recv()
 
     grad_in(3, bpb[...])
-    for ex in (q1[0], q1[1], q2[0], q2[1], f1[0], f1[1], s1, s2, s3, s4):
+    for h in range(2):
+        q_sent(0, h, q1, sq1, rx1)
+        q_sent(1, h, q2, sq2, rx2)
+        f_sent(0, h, f1, hid, rf1)
+    for ex in (s1, s2, s3, s4):
         ex[3]()
 
+    @pl.when(is_end)
+    def _():
+        meta_copy().wait_send()
+
     @pl.when(tm < n_tm - 1)
     def _():
         next_copy().wait_send()
@@ -433,13 +654,14 @@
         back_copy().wait_send()
 
     for h in range(2):
-        f2[h][2]()
+        f_received(1, h, f2)
         hop(hop2, hop1, rf2, h)
         mixed(2 * h, True)
         mixed(2 * h + 1, True)
     s5[2]()
-    for ex in (f2[0], f2[1], s5):
-        ex[3]()
+    s5[3]()
+    for h in range(2):
+        f_sent(1, h, f2, hop1, rf2)
 
 
 def finish(out_in, gin_in, fin, out_ref, gin_ref, gcw_ref, gcb_ref, gmw_ref, gmb_ref):
@@ -485,7 +707,11 @@
     ]
     scratch += [bf(2, 1024, 256)] * 8
     scratch += [fl(256, 128), fl(256, 128), fl(32, 128), fl(64, 128), fl(32, 128), fl(32, 128), fl(8, 128), fl(8, 128)]
-    scratch += [dma(8, n_space), dma(8, n_space), dma(5, n_e), dma(5, n_e), dma(4), dma(8)]
+    ints = pltpu.VMEM((16, 128), jnp.int32)
+    scratch += [ints, ints, bf(256, 512), bf(512, 256), bf(4, 256, 256), bf(4, 512, 256), bf(2, 512, 256), bf(2, 512, 256)]
+    scratch += [bf(4, 256, 256), bf(4, 256, 256)]
+    scratch += [dma(8, n_space), dma(8, n_space), dma(5, n_e), dma(5, n_e), dma(6), dma(8)]
+    scratch += [dma(4, 4), dma(4, 8), dma(4, 8)]
     out, gin, fin = pl.pallas_call(
         functools.partial(kernel, dims),
         out_shape=(

time: 113 us -> 113 us (level)
  no operation moved by 1% of the time
where the time goes in v4:
time: 113 us; the launch traced here: 111 us
  Pallas kernels  111 us (98%)
    pallas_call x1, Pallas kernels, body(): pl.pallas_call(functools.partial(kernel, dims), out_shape=(jax.ShapeDtype...  109 us

profile of v4, /device:TPU:1, one launch (start us, length us, event | category | flops | bytes accessed | tf_op | source)
XLA Modules:
  0.0 111.3 jit_solution(1843046317372924865)
XLA Ops:
  0.6 108.7 %shard_map.145 = (bf16[512,256]{1,0:T(8,128)(2,1)}, bf16[512,256]{1,0:T(8,128)(2,1)}, f32[256,128]{1,0:T(8,128)}) custom-call(bf16[512,256]{1,0:T(8,128)(2,1)} %bitcast.11, bf16[512,256]{1,0:T(8,128)(2,1)} %bitcast.12, bf16[2,8,128,128]{3,2,1,0:T(8,128)(2,1)} %adj_hbm.1, bf16[2,64,128]{2,1,0:T(8,128)(2,1)} %bitcast.13, f32[1,128]{1,0:T(1,128)} %bitcast.15, ...), custom_call_target="tpu_custom_call" | custom-call | tf_op jit(solution)/shard_map/pallas_call | solution.py:715
  109.4 1.9 %shard_map.146 = (bf16[512,256]{1,0:T(8,128)(2,1)}, bf16[512,256]{1,0:T(8,128)(2,1)}, f32[2,64,128]{2,1,0:T(8,128)}, f32[1,128]{1,0:T(1,128)}, f32[3,64,64]{2,1,0:T(8,128)}, /*index=5*/f32[1,64]{1,0:T(1,128)}) custom-call(bf16[512,256]{1,0:T(8,128)(2,1)} %get-tuple-element.15.out_in, bf16[512,256]{1,0:T(8,128)(2,1)} %get-tuple-element.16.gin_in, ...), custom_call_target="tpu_custom_call" | custom-call | tf_op jit(solution)/shard_map/pallas_call | solution.py:732

commit v5 on v4

--- a/solution.py
+++ b/solution.py
@@ -55,10 +55,10 @@
     dims,
     x_hbm, g_hbm, adj_hbm, convw_hbm, convb_hbm, mixw_hbm, mixb_hbm, send_hbm, cols_ref, counts_ref,
     out_ref, gin_ref, fin,
-    x_ref, g_ref, adj_ref, convw_ref, convb_ref, mixw_ref, mixb_ref, send_ref, xb, bpb, xt, gt, wt, wtt, mcat, mcatv, gm, gmt, dm, dmt, dlo, dlot,
+    xall, g_ref, adj_ref, convw_ref, convb_ref, mixw_ref, mixb_ref, send_ref, bpb, xt, gt, wt, wtt, mcat, mcatv, gm, gmt, dm, dmt, dlo, dlot,
     qg, qqg, filt, gate, hid, hidn, hop1, hop2, bp, part,
     sq1, sq2, sf1, sf2, rq1, rq2, rf1, rf2,
-    pay, ra, rb, rc, rd, sum_a, sum_b, sum_c,
+    pay, ra, rc, sum_b, sum_c,
     meta, metax, gx, gxt, far, pick, rx1, rx2, tsend, tback,
     ssem, rsem, assem, arsem, nsem, lsem, fsem, psem, xsem,
 ):
@@ -66,6 +66,8 @@
     me = lax.axis_index("space")
     tm = lax.axis_index("tm")
     dp = lax.axis_index("dp")
+    x_ref = xall.at[pl.ds(128, 512), :]
+    xb = xall.at[pl.ds(0, 128), :]
     z = lax.div(me, 4)
     y = lax.rem(me, 4)
     z_hi = lax.div(tm, 2)
@@ -83,11 +85,12 @@
     def space_dev(k):
         return {"space": k}
 
-    def e_dev(k):
-        return {"dp": lax.div(k, 2), "tm": z_hi * 2 + lax.rem(k, 2)}
-
-    def y_dev(k):
-        return {"space": z * 4 + k}
+    w = e * 4 + y
+    n_w = n_e * 4
+
+    def w_dev(k):
+        ek = lax.div(k, 4)
+        return {"dp": lax.div(ek, 2), "space": z * 4 + lax.rem(k, 4), "tm": z_hi * 2 + lax.rem(ek, 2)}
 
     def q_dev(k):
         return {"space": lax.rem(k, 4) * 4 + y, "tm": lax.div(k, 4) * 2 + core}
@@ -113,9 +116,9 @@
     def _(off):
         signal(space_dev(lax.rem(me + off, n_space)))
 
-    @pl.loop(1, n_e)
+    @pl.loop(1, n_w)
     def _(off):
-        signal(e_dev(lax.rem(e + off, n_e)))
+        signal(w_dev(lax.rem(w + off, n_w)))
 
     @pl.loop(0, 4)
     def _(k):
@@ -137,33 +140,34 @@
     f1 = halo(2, sf1, rf1)
     f2 = halo(3, sf2, rf2)
 
-    def by_distance(step):
-        far = 1 - lax.div(step, 2)
-        odd = lax.rem(lax.div(step + 1, 2), 2)
-        return 2 * lax.rem(lax.div(z, 2) + far, 2) + lax.rem(lax.rem(z, 2) + odd, 2)
+    def part_of(step, k):
+        sd = lax.rem(side + 1 + step, 2)
+        first = jnp.where(step == 0, 1 - side, 1 - lax.rem(z, 2))
+        return sd * 8 + lax.rem(first + lax.div(k, 4), 2) * 4 + lax.rem(y + k, 4)
+
+    def side_rows(step):
+        return pl.ds(pl.multiple_of(lax.rem(side + 1 + step, 2) * 512, 512), 512)
 
     def slot_block(ref, h, k):
         return ref.at[h, pl.ds(pl.multiple_of(k * SLOTS, SLOTS), SLOTS), :]
 
     def across(part):
-        return is_end & (lax.div(part, 8) != side)
+        return is_end & (part // 8 != side)
 
     def f_spread(ex, field, buf, h):
         copy = ex[h][0]
         lanes = slice(256 * h, 256 * (h + 1))
 
-        @pl.loop(0, 4)
+        @pl.loop(0, 2)
         def _(step):
-            zz = by_distance(step)
-
-            @pl.when(jnp.logical_not(across(zz * 4)))
+            @pl.when(jnp.logical_not(is_end & (step == 0)))
             def _():
-                at = pl.ds(pl.multiple_of(zz * 256, 256), 256)
+                at = side_rows(step)
                 buf[h, at, :] = nn(gmt[at, :], field[:, lanes]).astype(BF16)
 
-                @pl.loop(0, 4)
+                @pl.loop(0, 8)
                 def _(k):
-                    tgt = zz * 4 + lax.rem(y + k, 4)
+                    tgt = part_of(step, k)
 
                     @pl.when(tgt != me)
                     def _():
@@ -193,33 +197,31 @@
         def _():
             swap(i, h, field).wait_recv()
 
-            @pl.loop(0, 2)
-            def _(step):
-                zz = lax.rem(lax.rem(z, 2) + 1 + step, 2)
-                at = pl.ds(pl.multiple_of(zz * 256, 256), 256)
-                pick[2 * i + h, at, :] = nn(gxt[at, :], far[2 * i + h]).astype(BF16)
-
-                @pl.loop(0, 4)
-                def _(j):
-                    k = zz * 4 + lax.rem(y + j, 4)
-                    tgt = side * 8 + k
-
-                    @pl.when(tgt != me)
-                    def _():
-                        proxy_copy(i, h, recv, k, tgt).start()
+            pick[2 * i + h] = nn(gxt[...], far[2 * i + h]).astype(BF16)
+
+            @pl.loop(0, 8)
+            def _(j):
+                tgt = part_of(1, j)
+
+                @pl.when(tgt != me)
+                def _():
+                    proxy_copy(i, h, recv, tgt - side * 8, tgt).start()
 
             slot_block(recv, h, far_me)[...] = slot_block(pick, 2 * i + h, row_in_side)[...]
 
-    def f_received(i, h, ex):
+    def f_received(i, h, ex, recv, total):
         copy = ex[h][0]
-
-        @pl.loop(1, n_space)
-        def _(off):
-            frm = lax.rem(me + (n_space - off), n_space)
-
-            @pl.when(jnp.logical_not(is_end & (frm == far_me)))
-            def _():
-                copy(lax.rem(me + off, n_space), frm).wait_recv()
+        for half in range(2):
+            for k in range(8):
+                frm = 8 * half + k
+
+                @pl.when((frm != me) & jnp.logical_not(is_end & (frm == far_me)))
+                def _():
+                    copy(lax.rem(me + 1, n_space), frm).wait_recv()
+
+            at = slice(512 * half, 512 * (half + 1))
+            total = total + nn(dm[:, 256 + 512 * half : 768 + 512 * half], recv[h, at, :])
+        return total
 
     def f_sent(i, h, ex, field, recv):
         copy = ex[h][0]
@@ -249,25 +251,27 @@
             device_id=space_dev(end_z * 4 + lax.rem(s, 4)), device_id_type=MESH,
         )
 
-    def q_spread(i, ex, field, buf, rx, h):
+    def q_spread(i, ex, field, buf, rx, h, build=None):
         copy = ex[h][0]
         lanes = slice(256 * h, 256 * (h + 1))
 
-        @pl.loop(0, 4)
+        @pl.loop(0, 2)
         def _(step):
-            zz = by_distance(step)
-            at = pl.ds(pl.multiple_of(zz * 256, 256), 256)
+            if build is not None:
+                build(lax.rem(side + 1 + step, 2))
+            at = side_rows(step)
             buf[h, at, :] = nn(dmt[at, :], field[:, lanes]).astype(BF16)
 
-            @pl.loop(0, 4)
+            @pl.loop(0, 8)
             def _(k):
-                tgt = zz * 4 + lax.rem(y + k, 4)
-
-                @pl.when((zz != far_z) & (tgt != me))
+                tgt = part_of(step, k)
+                to_far = lax.div(tgt, 4) == far_z
+
+                @pl.when(jnp.logical_not(to_far) & (tgt != me))
                 def _():
                     copy(tgt, me).start()
 
-                @pl.when((zz == far_z) & (jnp.logical_not(is_end) | (tgt != far_me)))
+                @pl.when(to_far & (jnp.logical_not(is_end) | (tgt != far_me)))
                 def _():
                     collect_copy(i, h, buf, rx, tgt, row_in_side).start()
 
@@ -282,9 +286,7 @@
             device_id=space_dev(far_me), device_id_type=MESH,
         )
 
-    def q_received(i, h, ex, buf, rx):
-        copy = ex[h][0]
-
+    def q_collect(i, h, buf, rx):
         @pl.when(is_end)
         def _():
             @pl.loop(0, 8)
@@ -296,17 +298,24 @@
             tsend[2 * i + h] = nn(gx[...], rx[h]).astype(BF16)
             back_field(i, h).start()
 
-        @pl.loop(1, n_space)
-        def _(off):
-            frm = lax.rem(me + (n_space - off), n_space)
-
-            @pl.when(jnp.logical_not(across(frm)))
-            def _():
-                copy(lax.rem(me + off, n_space), frm).wait_recv()
+    def q_received(i, h, ex, recv, total):
+        copy = ex[h][0]
+        for half in range(2):
+            for k in range(8):
+                frm = 8 * half + k
+
+                @pl.when((frm != me) & jnp.logical_not(across(frm)))
+                def _():
+                    copy(lax.rem(me + 1, n_space), frm).wait_recv()
+
+            at = slice(512 * half, 512 * (half + 1))
+            total = total + nn(gm[:, at], recv[h, at, :])
 
         @pl.when(is_end)
         def _():
             back_field(i, h).wait_recv()
+
+        return total + tback[2 * i + h].astype(F32)
 
     def q_sent(i, h, ex, buf, rx):
         copy = ex[h][0]
@@ -336,7 +345,7 @@
 
     def next_copy():
         return pltpu.make_async_remote_copy(
-            src_ref=x_ref.at[pl.ds(384, 128), :], dst_ref=xb, send_sem=nsem.at[0], recv_sem=nsem.at[1],
+            src_ref=xall.at[pl.ds(512, 128), :], dst_ref=xb, send_sem=nsem.at[0], recv_sem=nsem.at[1],
             device_id={"tm": lax.rem(tm + 1, n_tm)}, device_id_type=MESH,
         )
 
@@ -346,10 +355,10 @@
             device_id={"tm": lax.rem(tm + n_tm - 1, n_tm)}, device_id_type=MESH,
         )
 
-    def tile_sum(r, b):
+    def tile_sum(r, b, own=False):
         total = None
         for k in range(4):
-            slot = k if b < 2 else 4 + k
+            slot = k if own else 4 + k
             hit = (cols_ref[r, slot] == b).astype(F32)
             term = adj_ref[r, slot].astype(F32) * hit
             total = term if total is None else total + term
@@ -359,11 +368,24 @@
     for p in range(4):
         gt[:, 128 * p : 128 * (p + 1)] = g_ref[128 * p : 128 * (p + 1), :].T
     loads[1].wait()
-    for b in range(2, 10):
-        for r in range(2):
-            block = tile_sum(r, b).astype(BF16)
-            dm[128 * r : 128 * (r + 1), 128 * b : 128 * (b + 1)] = block
-            dmt[128 * (b - 2) : 128 * (b - 1), 128 * r : 128 * (r + 1)] = block.T
+
+    def build(sd):
+        for k in range(4):
+            b = 4 * sd + k
+            at = pl.ds(pl.multiple_of(b * 128, 128), 128)
+            for r in range(2):
+                tile = tile_sum(r, b + 2).astype(BF16)
+                dm[128 * r : 128 * (r + 1), pl.ds(pl.multiple_of(256 + b * 128, 128), 128)] = tile
+                dmt[at, 128 * r : 128 * (r + 1)] = tile.T
+
+    loads[2].wait()
+    pl.semaphore_wait(barrier, n_space - 1 + n_w - 1 + 4 + 1)
+
+    @pl.when(tm < n_tm - 1)
+    def _():
+        next_copy().start()
+
+    q_spread(0, q1, gt, sq1, rx1, 0, build)
 
     own_slots = pl.ds(pl.multiple_of(me * SLOTS, SLOTS), SLOTS)
     for ref in (rq1, rq2, rf1, rf2):
@@ -379,54 +401,16 @@
     def _():
         tback[...] = jnp.zeros_like(tback)
 
-    for load in loads[2:]:
+    for load in loads[3:]:
         load.wait()
-    slot = lax.broadcasted_iota(jnp.int32, (1, SLOTS), 1)
-    for d in range(16):
-        picks = jnp.where(slot < counts_ref[0, d], send_ref[d : d + 1, :], -1)
-        meta[d : d + 1, :] = jnp.concatenate([picks, picks], 1)
-    pl.semaphore_wait(barrier, n_space - 1 + n_e - 1 + 4 + 1)
-
-    @pl.when(is_end)
-    def _():
-        meta_copy().start()
-
-    for h in range(2):
-        q_spread(0, q1, gt, sq1, rx1, h)
-
-    @pl.when(tm < n_tm - 1)
-    def _():
-        next_copy().start()
 
     @pl.when(tm == 0)
     def _():
-        xb[...] = jnp.zeros_like(xb)
+        xb[...] = jnp.zeros((128, 256), BF16)
 
     @pl.when(tm == n_tm - 1)
     def _():
         bpb[...] = jnp.zeros_like(bpb)
-
-    for b in range(2):
-        for r in range(2):
-            total = tile_sum(r, b)
-            high = total.astype(BF16)
-            low = (total - high.astype(F32)).astype(BF16)
-            here = slice(128 * r, 128 * (r + 1)), slice(128 * b, 128 * (b + 1))
-            dm[here] = high
-            dlo[here] = low
-            dlot[128 * b : 128 * (b + 1), 128 * r : 128 * (r + 1)] = high.T
-            dlot[128 * b : 128 * (b + 1), 256 + 128 * r : 256 + 128 * (r + 1)] = low.T
-
-    sensor = lax.broadcasted_iota(jnp.int32, (256, 128), 0)
-    low_row = lax.broadcasted_iota(jnp.int32, (1, 128), 1) < 64
-
-    def select(first, second):
-        return (sensor == jnp.where(low_row, first, second)).astype(F32).astype(BF16)
-
-    for m in range(8):
-        sel = select(meta[2 * m : 2 * m + 1, :], meta[2 * m + 1 : 2 * m + 2, :])
-        gm[:, 128 * m : 128 * (m + 1)] = sel
-        gmt[128 * m : 128 * (m + 1), :] = sel.T
 
     zero = jnp.zeros((64, 64), F32)
 
@@ -447,14 +431,10 @@
     for p in range(4):
         xt[:, 128 * (p + 1) : 128 * (p + 2)] = x_ref[128 * p : 128 * (p + 1), :].T
 
-    @pl.when(tm > 0)
-    def _():
-        next_copy().wait_recv()
-
-    xt[:, 0:128] = xb[...].T
     b = convb_ref[...]
     bias = jnp.concatenate([b[:, :64], b[:, :64], b[:, 64:], b[:, 64:]], 1)
-    for p in range(4):
+
+    def conv(p):
         lanes = slice(128 * p, 128 * (p + 1))
         pre = nt(xt[:, 128 * p : 128 * p + 256], wt[...]) + bias
         f = jnp.tanh(pre[:, :128])
@@ -463,8 +443,52 @@
         gate[:, lanes] = s
         hid[:, lanes] = (f * s).astype(BF16)
 
-    for h in range(2):
-        f_swap(0, h, hid)
+    for p in (2, 3):
+        conv(p)
+    f_swap(0, 1, hid)
+    slot = lax.broadcasted_iota(jnp.int32, (1, SLOTS), 1)
+    for d in range(16):
+        picks = jnp.where(slot < counts_ref[0, d], send_ref[d : d + 1, :], -1)
+        meta[d : d + 1, :] = jnp.concatenate([picks, picks], 1)
+
+    @pl.when(is_end)
+    def _():
+        meta_copy().start()
+
+    q_spread(0, q1, gt, sq1, rx1, 1)
+    conv(1)
+
+    sensor = lax.broadcasted_iota(jnp.int32, (256, 128), 0)
+    low_row = lax.broadcasted_iota(jnp.int32, (1, 128), 1) < 64
+
+    def select(first, second):
+        return (sensor == jnp.where(low_row, first, second)).astype(F32).astype(BF16)
+
+    for m in range(8):
+        sel = select(meta[2 * m : 2 * m + 1, :], meta[2 * m + 1 : 2 * m + 2, :])
+        gm[:, 128 * m : 128 * (m + 1)] = sel
+        gmt[128 * m : 128 * (m + 1), :] = sel.T
+
+    f_spread(f1, hid, sf1, 1)
+
+    @pl.when(tm > 0)
+    def _():
+        next_copy().wait_recv()
+
+    xt[:, 0:128] = xb[...].T
+    conv(0)
+    f_swap(0, 0, hid)
+
+    for b in range(2):
+        for r in range(2):
+            total = tile_sum(r, b, True)
+            high = total.astype(BF16)
+            low = (total - high.astype(F32)).astype(BF16)
+            here = slice(128 * r, 128 * (r + 1)), slice(128 * b, 128 * (b + 1))
+            dm[here] = high
+            dlo[here] = low
+            dlot[128 * b : 128 * (b + 1), 128 * r : 128 * (r + 1)] = high.T
+            dlot[128 * b : 128 * (b + 1), 256 + 128 * r : 256 + 128 * (r + 1)] = low.T
 
     @pl.when(is_end)
     def _():
@@ -475,24 +499,37 @@
             gx[:, 128 * m : 128 * (m + 1)] = sel
             gxt[128 * m : 128 * (m + 1), :] = sel.T
 
+    def own_back(field, h):
+        grad = field[:, 256 * h : 256 * (h + 1)]
+        return nn(dlot[:, :256], grad) + nn(dlot[:, 256:], grad)
+
+    q_collect(0, 0, sq1, rx1)
+    f_proxy(0, 1, hid, rf1)
+    q_collect(0, 1, sq1, rx1)
     for h in range(2):
+        own = own_back(gt, h)
+        qg[:, 256 * h : 256 * (h + 1)] = q_received(0, h, q1, rq1, own).astype(BF16)
+        q_spread(1, q2, qg, sq2, rx2, h)
+
+    def hop(i, h, ex, src, dst, recv):
         lanes = slice(256 * h, 256 * (h + 1))
-        q_received(0, h, q1, sq1, rx1)
-        grad = gt[:, lanes]
-        own = nn(dlot[:, :256], grad) + nn(dlot[:, 256:], grad)
-        own = own + tback[h].astype(F32)
-        qg[:, lanes] = (own + nn(gm[...], rq1[h])).astype(BF16)
-        q_spread(1, q2, qg, sq2, rx2, h)
-
-    for h in range(2):
-        f_spread(f1, hid, sf1, h)
-        f_proxy(0, h, hid, rf1)
+        field = src[:, lanes]
+        own = nn(dm[:, :256], field) + nn(dlo[...], field)
+        dst[:, lanes] = f_received(i, h, ex, recv, own).astype(BF16)
+
+    f_spread(f1, hid, sf1, 0)
+    f_proxy(0, 0, hid, rf1)
     for p in range(4):
         lanes = slice(128 * p, 128 * (p + 1))
         hidn[lanes, :] = hid[:, lanes].T
     gsum = jnp.zeros((1, 128), F32)
     for p in range(4):
         gsum = gsum + jnp.sum(gt[:, 128 * p : 128 * (p + 1)].astype(F32), axis=0, keepdims=True)
+    hop(0, 1, f1, hid, hop1, rf1)
+    f_swap(1, 1, hop1)
+    f_spread(f2, hop1, sf2, 1)
+    for h in range(2):
+        q_collect(1, h, sq2, rx2)
 
     low_lanes = lax.broadcasted_iota(jnp.int32, (64, 128), 1) < 64
 
@@ -503,22 +540,18 @@
         return pltpu.roll(a[:64], 64, 1) + a[64:]
 
     bsum = jnp.zeros((1, 256), F32)
-    accs = [None] * 5
+    accs = [None] * 2
 
     def add(i, term):
         accs[i] = term if accs[i] is None else accs[i] + term
 
     for h in range(2):
-        lanes = slice(256 * h, 256 * (h + 1))
-        q_received(1, h, q2, sq2, rx2)
-        grad = qg[:, lanes]
-        own = nn(dlot[:, :256], grad) + nn(dlot[:, 256:], grad)
-        own = own + tback[2 + h].astype(F32)
-        qqg[:, lanes] = (own + nn(gm[...], rq2[h])).astype(BF16)
+        own = own_back(qg, h)
+        qqg[:, 256 * h : 256 * (h + 1)] = q_received(1, h, q2, rq2, own).astype(BF16)
         for p in (2 * h, 2 * h + 1):
             lanes = slice(128 * p, 128 * (p + 1))
-            three = (gt[:, lanes], qg[:, lanes], qqg[:, lanes])
-            bh = nn(jnp.concatenate(three, 1), mcatv[...])
+            three = jnp.concatenate([gt[:, lanes], qg[:, lanes], qqg[:, lanes]], 1)
+            bh = nn(three, mcatv[...])
             f = filt[:, lanes]
             s = gate[:, lanes]
             gf = (bh * (1.0 - f * f) * s).astype(BF16)
@@ -536,11 +569,10 @@
                 ],
                 1,
             )
-            for k in range(3):
-                add(k, nn(hidn[lanes, :], three[k]))
-            wide = bp[:, 256 * p : 256 * (p + 1)]
-            add(3, nn(xb[...] if p == 0 else x_ref[128 * (p - 1) : 128 * p, :], wide))
-            add(4, nn(x_ref[lanes, :], wide))
+            add(0, nn(hidn[lanes, :], three))
+            add(1, nn(xall[128 * p : 128 * p + 256, :], bp[:, 256 * p : 256 * (p + 1)]))
+        if h == 0:
+            f_proxy(1, 1, hop1, rf2)
     row = lax.broadcasted_iota(jnp.int32, (64, 128), 0)
     f_sum = bsum[:, :128]
     g_sum = bsum[:, 128:]
@@ -548,19 +580,17 @@
     g_sum = g_sum + pltpu.roll(g_sum, 64, 1)
     o_sum = gsum + pltpu.roll(gsum, 64, 1)
     extra = jnp.where(row == 0, f_sum, jnp.where(row == 1, g_sum, jnp.where(row == 2, o_sum, 0.0)))
-    pay[0:64, :] = jnp.where(low_lanes, diag_low(accs[0]), diag_high(accs[1]))
-    pay[64:128, :] = jnp.where(low_lanes, diag_low(accs[2]), extra)
+    pay[0:64, :] = jnp.where(low_lanes, diag_low(accs[0][:, :128]), diag_high(accs[0][:, 128:256]))
+    pay[64:128, :] = jnp.where(low_lanes, diag_low(accs[0][:, 256:]), extra)
     for tap in range(2):
-        acc = accs[3 + tap]
+        acc = accs[1][128 * tap : 128 * (tap + 1)]
         pay[128 + 64 * tap : 192 + 64 * tap, :] = jnp.where(
             low_lanes, diag_low(acc[:, :128]), diag_high(acc[:, 128:])
         )
 
-    s1 = exchange(e, n_e, e_dev, rows(pay, 32), rows(ra, 32), assem.at[0], arsem.at[0])
-    s2 = exchange(y, 4, y_dev, rows(sum_a, 8), rows(rb, 8), assem.at[1], arsem.at[1])
-    s3 = exchange(q, 8, q_dev, lambda k: sum_b, rows(rc, 8), assem.at[2], arsem.at[2])
-    s4 = exchange(y, 4, y_dev, lambda k: sum_c, rows(rd, 8), assem.at[3], arsem.at[3])
-    s5 = exchange(e, n_e, e_dev, lambda k: rd, rows(fin, 32), assem.at[4], arsem.at[4])
+    s1 = exchange(w, n_w, w_dev, rows(pay, 8), rows(ra, 8), assem.at[0], arsem.at[0])
+    s2 = exchange(q, 8, q_dev, lambda k: sum_b, rows(rc, 8), assem.at[1], arsem.at[1])
+    s3 = exchange(w, n_w, w_dev, lambda k: sum_c, rows(fin, 8), assem.at[2], arsem.at[2])
 
     def total_of(ref, count, size):
         total = ref[0:size, :]
@@ -571,36 +601,20 @@
     def place(k, size):
         return pl.ds(pl.multiple_of(k * size, size), size)
 
-    ra[place(e, 32), :] = pay[place(e, 32), :]
+    ra[place(w, 8), :] = pay[place(w, 8), :]
     s1[1]()
 
-    def grad_in(p, nxt):
+    def grad_in(p):
         lanes = slice(128 * p, 128 * (p + 1))
-        here = nt(wtt[128:, :], bp[:, 256 * p : 256 * (p + 1)])
-        gin_ref[lanes, :] = (g_ref[lanes, :].astype(F32) + here + nt(wtt[:128, :], nxt)).astype(BF16)
+        if p < 3:
+            here = nt(jnp.concatenate([wtt[128:, :], wtt[:128, :]], 1), bp[:, 256 * p : 256 * p + 512])
+        else:
+            here = nt(wtt[128:, :], bp[:, 768:]) + nt(wtt[:128, :], bpb[...])
+        gin_ref[lanes, :] = (g_ref[lanes, :].astype(F32) + here).astype(BF16)
 
     mb = mixb_ref[...]
     mb = jnp.broadcast_to(jnp.concatenate([mb, mb], 1), (128, 128)).T
     mb = jnp.concatenate([mb, mb], 1)
-
-    for p in range(3):
-        grad_in(p, bp[:, 256 * (p + 1) : 256 * (p + 2)])
-
-    s1[2]()
-    sum_a[...] = total_of(ra, n_e, 32)
-    rb[place(y, 8), :] = sum_a[place(y, 8), :]
-    s2[1]()
-    s2[2]()
-    total = total_of(rb, 4, 8)
-    sum_b[...] = total
-    rc[place(q, 8), :] = total
-    s3[1]()
-
-    def hop(dst, src, recv, h):
-        lanes = slice(256 * h, 256 * (h + 1))
-        field = src[:, lanes]
-        own = nn(dm[:, :256], field) + nn(dlo[...], field)
-        dst[:, lanes] = (own + nn(dm[:, 256:], recv[h])).astype(BF16)
 
     def mixed(p, last):
         lanes = slice(128 * p, 128 * (p + 1))
@@ -608,24 +622,25 @@
             here = nt(mcat[:, 256:], hop2[:, lanes])
             out_ref[lanes, :] = (part[lanes, :] + here).astype(BF16)
         else:
-            here = nt(mcat[:, :128], hid[:, lanes]) + nt(mcat[:, 128:256], hop1[:, lanes])
+            here = nt(mcat[:, :256], jnp.concatenate([hid[:, lanes], hop1[:, lanes]], 1))
             part[lanes, :] = x_ref[lanes, :].astype(F32) + mb + here
 
-    for h in range(2):
-        f_received(0, h, f1)
-        hop(hop1, hid, rf1, h)
-        f_swap(1, h, hop1)
-        f_spread(f2, hop1, sf2, h)
+    hop(0, 0, f1, hid, hop1, rf1)
+    f_swap(1, 0, hop1)
+    f_spread(f2, hop1, sf2, 0)
+    s1[2]()
+    total = total_of(ra, n_w, 8)
+    sum_b[...] = total
+    rc[place(q, 8), :] = total
+    s2[1]()
     f_proxy(1, 0, hop1, rf2)
-    s3[2]()
+    for p in range(3):
+        grad_in(p)
+    s2[2]()
     total = total_of(rc, 8, 8) * scale
     sum_c[...] = total
-    rd[place(y, 8), :] = total
-    s4[1]()
-    f_proxy(1, 1, hop1, rf2)
-    s4[2]()
-    fin[place(e, 32), :] = rd[...]
-    s5[1]()
+    fin[place(w, 8), :] = total
+    s3[1]()
     for p in range(4):
         mixed(p, False)
 
@@ -633,13 +648,13 @@
     def _():
         back_copy().wait_recv()
 
-    grad_in(3, bpb[...])
+    grad_in(3)
     for h in range(2):
         q_sent(0, h, q1, sq1, rx1)
         q_sent(1, h, q2, sq2, rx2)
         f_sent(0, h, f1, hid, rf1)
-    for ex in (s1, s2, s3, s4):
-        ex[3]()
+    s1[3]()
+    s2[3]()
 
     @pl.when(is_end)
     def _():
@@ -653,13 +668,12 @@
     def _():
         back_copy().wait_send()
 
-    for h in range(2):
-        f_received(1, h, f2)
-        hop(hop2, hop1, rf2, h)
+    for h in (1, 0):
+        hop(1, h, f2, hop1, hop2, rf2)
         mixed(2 * h, True)
         mixed(2 * h + 1, True)
-    s5[2]()
-    s5[3]()
+    s3[2]()
+    s3[3]()
     for h in range(2):
         f_sent(1, h, f2, hop1, rf2)
 
@@ -698,19 +712,19 @@
         return pltpu.SemaphoreType.DMA(shape)
 
     scratch = [
-        bf(512, 256), bf(512, 256), bf(2, 8, 128, 128), bf(2, 64, 128), fl(1, 128), bf(3, 64, 64), fl(1, 64),
-        pltpu.VMEM((16, SLOTS), jnp.int32), bf(128, 256), bf(256, 256), bf(256, 640), bf(256, 512),
+        bf(640, 256), bf(512, 256), bf(2, 8, 128, 128), bf(2, 64, 128), fl(1, 128), bf(3, 64, 64), fl(1, 64),
+        pltpu.VMEM((16, SLOTS), jnp.int32), bf(256, 256), bf(256, 640), bf(256, 512),
         bf(256, 256), bf(256, 256), bf(128, 384), bf(384, 128),
         bf(256, 1024), bf(1024, 256), bf(256, 1280), bf(1024, 256), bf(256, 256), bf(256, 512),
         bf(256, 512), bf(256, 512), fl(256, 512), fl(256, 512), bf(256, 512), bf(512, 256),
         bf(256, 512), bf(256, 512), bf(256, 1024), fl(512, 256),
     ]
     scratch += [bf(2, 1024, 256)] * 8
-    scratch += [fl(256, 128), fl(256, 128), fl(32, 128), fl(64, 128), fl(32, 128), fl(32, 128), fl(8, 128), fl(8, 128)]
+    scratch += [fl(256, 128), fl(256, 128), fl(64, 128), fl(8, 128), fl(8, 128)]
     ints = pltpu.VMEM((16, 128), jnp.int32)
     scratch += [ints, ints, bf(256, 512), bf(512, 256), bf(4, 256, 256), bf(4, 512, 256), bf(2, 512, 256), bf(2, 512, 256)]
     scratch += [bf(4, 256, 256), bf(4, 256, 256)]
-    scratch += [dma(8, n_space), dma(8, n_space), dma(5, n_e), dma(5, n_e), dma(6), dma(8)]
+    scratch += [dma(8, n_space), dma(8, n_space), dma(3, 4 * n_e), dma(3, 4 * n_e), dma(6), dma(8)]
     scratch += [dma(4, 4), dma(4, 8), dma(4, 8)]
     out, gin, fin = pl.pallas_call(
         functools.partial(kernel, dims),

time: 113 us -> 102 us (0.903); the launches traced: 111 us -> 102 us
  Pallas kernels: 111 us -> 101 us
    pallas_call x1, Pallas kernels: 109 us -> 98.9 us  [body(): pl.pallas_call(functools.partial(kernel, dims), out_shape=(jax.ShapeDtype...]
where the time goes in v5:
time: 102 us
  Pallas kernels  101 us (99%)
    pallas_call x1, Pallas kernels, body(): pl.pallas_call(functools.partial(kernel, dims), out_shape=(jax.ShapeDtype...  98.9 us

profile of v5, /device:TPU:1, one launch (start us, length us, event | category | flops | bytes accessed | tf_op | source)
XLA Modules:
  0.0 101.5 jit_solution(14058227303131921722)
XLA Ops:
  0.6 98.9 %shard_map.145 = (bf16[512,256]{1,0:T(8,128)(2,1)}, bf16[512,256]{1,0:T(8,128)(2,1)}, f32[256,128]{1,0:T(8,128)}) custom-call(bf16[512,256]{1,0:T(8,128)(2,1)} %bitcast.11, bf16[512,256]{1,0:T(8,128)(2,1)} %bitcast.12, bf16[2,8,128,128]{3,2,1,0:T(8,128)(2,1)} %adj_hbm.1, bf16[2,64,128]{2,1,0:T(8,128)(2,1)} %bitcast.13, f32[1,128]{1,0:T(1,128)} %bitcast.15, ...), custom_call_target="tpu_custom_call" | custom-call | tf_op jit(solution)/shard_map/pallas_call | solution.py:729
  99.6 1.9 %shard_map.146 = (bf16[512,256]{1,0:T(8,128)(2,1)}, bf16[512,256]{1,0:T(8,128)(2,1)}, f32[2,64,128]{2,1,0:T(8,128)}, f32[1,128]{1,0:T(1,128)}, f32[3,64,64]{2,1,0:T(8,128)}, /*index=5*/f32[1,64]{1,0:T(1,128)}) custom-call(bf16[512,256]{1,0:T(8,128)(2,1)} %get-tuple-element.15.out_in, bf16[512,256]{1,0:T(8,128)(2,1)} %get-tuple-element.16.gin_in, ...), custom_call_target="tpu_custom_call" | custom-call | tf_op jit(solution)/shard_map/pallas_call | solution.py:746

commit v6 on v5

--- a/solution.py
+++ b/solution.py
@@ -54,13 +54,14 @@
 def kernel(
     dims,
     x_hbm, g_hbm, adj_hbm, convw_hbm, convb_hbm, mixw_hbm, mixb_hbm, send_hbm, cols_ref, counts_ref,
+    out_hbm, gin_hbm, fin_hbm,
     out_ref, gin_ref, fin,
     xall, g_ref, adj_ref, convw_ref, convb_ref, mixw_ref, mixb_ref, send_ref, bpb, xt, gt, wt, wtt, mcat, mcatv, gm, gmt, dm, dmt, dlo, dlot,
     qg, qqg, filt, gate, hid, hidn, hop1, hop2, bp, part,
     sq1, sq2, sf1, sf2, rq1, rq2, rf1, rf2,
     pay, ra, rc, sum_b, sum_c,
     meta, metax, gx, gxt, far, pick, rx1, rx2, tsend, tback,
-    ssem, rsem, assem, arsem, nsem, lsem, fsem, psem, xsem,
+    ssem, rsem, assem, arsem, nsem, lsem, fsem, psem, xsem, osem,
 ):
     n_space, n_dp, n_tm, scale = dims
     me = lax.axis_index("space")
@@ -109,6 +110,11 @@
     ]
     for load in loads:
         load.start()
+
+    parts = [(gin_ref, gin_hbm)]
+    parts += [(ref.at[pl.ds(256 * h, 256), :], dst.at[pl.ds(256 * h, 256), :]) for h in range(2) for ref, dst in ((out_ref, out_hbm),)]
+    parts += [(fin, fin_hbm)]
+    stores = [pltpu.make_async_copy(src, dst, osem.at[i]) for i, (src, dst) in enumerate(parts)]
 
     barrier = pltpu.get_barrier_semaphore()
 
@@ -627,13 +633,12 @@
 
     hop(0, 0, f1, hid, hop1, rf1)
     f_swap(1, 0, hop1)
-    f_spread(f2, hop1, sf2, 0)
     s1[2]()
     total = total_of(ra, n_w, 8)
     sum_b[...] = total
     rc[place(q, 8), :] = total
     s2[1]()
-    f_proxy(1, 0, hop1, rf2)
+    f_spread(f2, hop1, sf2, 0)
     for p in range(3):
         grad_in(p)
     s2[2]()
@@ -641,6 +646,7 @@
     sum_c[...] = total
     fin[place(w, 8), :] = total
     s3[1]()
+    f_proxy(1, 0, hop1, rf2)
     for p in range(4):
         mixed(p, False)
 
@@ -649,6 +655,7 @@
         back_copy().wait_recv()
 
     grad_in(3)
+    stores[0].start()
     for h in range(2):
         q_sent(0, h, q1, sq1, rx1)
         q_sent(1, h, q2, sq2, rx2)
@@ -672,10 +679,14 @@
         hop(1, h, f2, hop1, hop2, rf2)
         mixed(2 * h, True)
         mixed(2 * h + 1, True)
+        stores[1 + h].start()
     s3[2]()
+    stores[3].start()
     s3[3]()
     for h in range(2):
         f_sent(1, h, f2, hop1, rf2)
+    for store in stores:
+        store.wait()
 
 
 def finish(out_in, gin_in, fin, out_ref, gin_ref, gcw_ref, gcb_ref, gmw_ref, gmb_ref):
@@ -712,6 +723,7 @@
         return pltpu.SemaphoreType.DMA(shape)
 
     scratch = [
+        bf(512, 256), bf(512, 256), fl(256, 128),
         bf(640, 256), bf(512, 256), bf(2, 8, 128, 128), bf(2, 64, 128), fl(1, 128), bf(3, 64, 64), fl(1, 64),
         pltpu.VMEM((16, SLOTS), jnp.int32), bf(256, 256), bf(256, 640), bf(256, 512),
         bf(256, 256), bf(256, 256), bf(128, 384), bf(384, 128),
@@ -725,7 +737,7 @@
     scratch += [ints, ints, bf(256, 512), bf(512, 256), bf(4, 256, 256), bf(4, 512, 256), bf(2, 512, 256), bf(2, 512, 256)]
     scratch += [bf(4, 256, 256), bf(4, 256, 256)]
     scratch += [dma(8, n_space), dma(8, n_space), dma(3, 4 * n_e), dma(3, 4 * n_e), dma(6), dma(8)]
-    scratch += [dma(4, 4), dma(4, 8), dma(4, 8)]
+    scratch += [dma(4, 4), dma(4, 8), dma(4, 8), dma(4)]
     out, gin, fin = pl.pallas_call(
         functools.partial(kernel, dims),
         out_shape=(
@@ -734,7 +746,7 @@
             jax.ShapeDtypeStruct((256, 128), F32),
         ),
         in_specs=[hbm] * 8 + [smem] * 2,
-        out_specs=(vmem,) * 3,
+        out_specs=(hbm,) * 3,
         scratch_shapes=scratch,
         compiler_params=pltpu.CompilerParams(
             collective_id=0, has_side_effects=True, vmem_limit_bytes=60 * 2**20

time: 102 us -> 98.7 us (0.968)
  Pallas kernels: 101 us -> 97.9 us
    pallas_call x1, Pallas kernels: 98.9 us -> 96 us  [body(): pl.pallas_call(functools.partial(kernel, dims), out_shape=(jax.ShapeDtype...]
where the time goes in v6:
time: 98.7 us; the launch traced here: 98.6 us
  Pallas kernels  97.9 us (99%)
    pallas_call x1, Pallas kernels, body(): pl.pallas_call(functools.partial(kernel, dims), out_shape=(jax.ShapeDtype...  96 us

profile of v6, /device:TPU:1, one launch (start us, length us, event | category | flops | bytes accessed | tf_op | source)
XLA Modules:
  0.0 98.6 jit_solution(13470766092595992438)
XLA Ops:
  0.6 96.0 %shard_map.145 = (bf16[512,256]{1,0:T(8,128)(2,1)}, bf16[512,256]{1,0:T(8,128)(2,1)}, f32[256,128]{1,0:T(8,128)}) custom-call(bf16[512,256]{1,0:T(8,128)(2,1)} %bitcast.11, bf16[512,256]{1,0:T(8,128)(2,1)} %bitcast.12, bf16[2,8,128,128]{3,2,1,0:T(8,128)(2,1)} %adj_hbm.1, bf16[2,64,128]{2,1,0:T(8,128)(2,1)} %bitcast.13, f32[1,128]{1,0:T(1,128)} %bitcast.15, ...), custom_call_target="tpu_custom_call" | custom-call | tf_op jit(solution)/shard_map/pallas_call | solution.py:741
  96.6 1.9 %shard_map.146 = (bf16[512,256]{1,0:T(8,128)(2,1)}, bf16[512,256]{1,0:T(8,128)(2,1)}, f32[2,64,128]{2,1,0:T(8,128)}, f32[1,128]{1,0:T(1,128)}, f32[3,64,64]{2,1,0:T(8,128)}, /*index=5*/f32[1,64]{1,0:T(1,128)}) custom-call(bf16[512,256]{1,0:T(8,128)(2,1)} %get-tuple-element.15.out_in, bf16[512,256]{1,0:T(8,128)(2,1)} %get-tuple-element.16.gin_in, ...), custom_call_target="tpu_custom_call" | custom-call | tf_op jit(solution)/shard_map/pallas_call | solution.py:758

commit v7 on v6

--- a/solution.py
+++ b/solution.py
@@ -56,7 +56,7 @@
     x_hbm, g_hbm, adj_hbm, convw_hbm, convb_hbm, mixw_hbm, mixb_hbm, send_hbm, cols_ref, counts_ref,
     out_hbm, gin_hbm, fin_hbm,
     out_ref, gin_ref, fin,
-    xall, g_ref, adj_ref, convw_ref, convb_ref, mixw_ref, mixb_ref, send_ref, bpb, xt, gt, wt, wtt, mcat, mcatv, gm, gmt, dm, dmt, dlo, dlot,
+    xall, g_ref, adj_ref, convw_ref, convb_ref, mixw_ref, mixb_ref, send_ref, bps, bpb, xt, gt, wt, wtt, mcat, mcatv, gm, gmt, dm, dmt, dlo, dlot,
     qg, qqg, filt, gate, hid, hidn, hop1, hop2, bp, part,
     sq1, sq2, sf1, sf2, rq1, rq2, rf1, rf2,
     pay, ra, rc, sum_b, sum_c,
@@ -357,7 +357,7 @@
 
     def back_copy():
         return pltpu.make_async_remote_copy(
-            src_ref=bp.at[:, pl.ds(0, 256)], dst_ref=bpb, send_sem=nsem.at[2], recv_sem=nsem.at[3],
+            src_ref=bps, dst_ref=bpb, send_sem=nsem.at[2], recv_sem=nsem.at[3],
             device_id={"tm": lax.rem(tm + n_tm - 1, n_tm)}, device_id_type=MESH,
         )
 
@@ -516,6 +516,8 @@
         own = own_back(gt, h)
         qg[:, 256 * h : 256 * (h + 1)] = q_received(0, h, q1, rq1, own).astype(BF16)
         q_spread(1, q2, qg, sq2, rx2, h)
+        if h == 0:
+            f_spread(f1, hid, sf1, 0)
 
     def hop(i, h, ex, src, dst, recv):
         lanes = slice(256 * h, 256 * (h + 1))
@@ -523,7 +525,6 @@
         own = nn(dm[:, :256], field) + nn(dlo[...], field)
         dst[:, lanes] = f_received(i, h, ex, recv, own).astype(BF16)
 
-    f_spread(f1, hid, sf1, 0)
     f_proxy(0, 0, hid, rf1)
     for p in range(4):
         lanes = slice(128 * p, 128 * (p + 1))
@@ -565,6 +566,8 @@
             bp[:, 256 * p : 256 * p + 128] = gf
             bp[:, 256 * p + 128 : 256 * (p + 1)] = gg
             if p == 0:
+                bps[...] = nt(wtt[:128, :], bp[:, :256]).astype(BF16)
+
                 @pl.when(tm > 0)
                 def _():
                     back_copy().start()
@@ -615,7 +618,7 @@
         if p < 3:
             here = nt(jnp.concatenate([wtt[128:, :], wtt[:128, :]], 1), bp[:, 256 * p : 256 * p + 512])
         else:
-            here = nt(wtt[128:, :], bp[:, 768:]) + nt(wtt[:128, :], bpb[...])
+            here = nt(wtt[128:, :], bp[:, 768:]) + bpb[...].astype(F32)
         gin_ref[lanes, :] = (g_ref[lanes, :].astype(F32) + here).astype(BF16)
 
     mb = mixb_ref[...]
@@ -725,7 +728,7 @@
     scratch = [
         bf(512, 256), bf(512, 256), fl(256, 128),
         bf(640, 256), bf(512, 256), bf(2, 8, 128, 128), bf(2, 64, 128), fl(1, 128), bf(3, 64, 64), fl(1, 64),
-        pltpu.VMEM((16, SLOTS), jnp.int32), bf(256, 256), bf(256, 640), bf(256, 512),
+        pltpu.VMEM((16, SLOTS), jnp.int32), bf(128, 256), bf(128, 256), bf(256, 640), bf(256, 512),
         bf(256, 256), bf(256, 256), bf(128, 384), bf(384, 128),
         bf(256, 1024), bf(1024, 256), bf(256, 1280), bf(1024, 256), bf(256, 256), bf(256, 512),
         bf(256, 512), bf(256, 512), fl(256, 512), fl(256, 512), bf(256, 512), bf(512, 256),

time: 98.7 us -> 97.9 us (level)
  no operation moved by 1% of the time
where the time goes in v7:
time: 97.9 us; the launch traced here: 97.7 us
  Pallas kernels  97.1 us (99%)
    pallas_call x1, Pallas kernels, body(): pl.pallas_call(functools.partial(kernel, dims), out_shape=(jax.ShapeDtype...  95.2 us

profile of v7, /device:TPU:1, one launch (start us, length us, event | category | flops | bytes accessed | tf_op | source)
XLA Modules:
  0.0 97.7 jit_solution(17375614364754089839)
XLA Ops:
  0.6 95.2 %shard_map.145 = (bf16[512,256]{1,0:T(8,128)(2,1)}, bf16[512,256]{1,0:T(8,128)(2,1)}, f32[256,128]{1,0:T(8,128)}) custom-call(bf16[512,256]{1,0:T(8,128)(2,1)} %bitcast.11, bf16[512,256]{1,0:T(8,128)(2,1)} %bitcast.12, bf16[2,8,128,128]{3,2,1,0:T(8,128)(2,1)} %adj_hbm.1, bf16[2,64,128]{2,1,0:T(8,128)(2,1)} %bitcast.13, f32[1,128]{1,0:T(1,128)} %bitcast.15, ...), custom_call_target="tpu_custom_call" | custom-call | tf_op jit(solution)/shard_map/pallas_call | solution.py:744
  95.8 1.9 %shard_map.146 = (bf16[512,256]{1,0:T(8,128)(2,1)}, bf16[512,256]{1,0:T(8,128)(2,1)}, f32[2,64,128]{2,1,0:T(8,128)}, f32[1,128]{1,0:T(1,128)}, f32[3,64,64]{2,1,0:T(8,128)}, /*index=5*/f32[1,64]{1,0:T(1,128)}) custom-call(bf16[512,256]{1,0:T(8,128)(2,1)} %get-tuple-element.15.out_in, bf16[512,256]{1,0:T(8,128)(2,1)} %get-tuple-element.16.gin_in, ...), custom_call_target="tpu_custom_call" | custom-call | tf_op jit(solution)/shard_map/pallas_call | solution.py:761
